TPU v7x, 32 devices: a whole 2x2x4 slice. The times are simulated.
32 devices in a mesh: dp: 8 (over y, x, core), tensor: 4 (over z).
Axes of the slice: x: 2, y: 2, z: 4, core: 2. Of those that a mesh axis runs over, the one named last changes fastest.
Arguments:
- hidden_states: float32 [2048, 1024], P('dp'), may hold values from -6 to 6
- output_cotangent: float32 [2048, 1024], P('dp'), may hold values from -6 to 6
- routes: int32 [2048, 8], P('dp'), may hold values from 0 to 31, all different within a row; in each aligned block of 256 rows (0 to 255, 256 to 511, ...) at most 96 rows name the same one
- attention_gain: float32 [2, 1024], replicated, may hold values from 0.5 to 1.5
- query_weight: bfloat16 [2, 1024, 1024], P(None, None, 'tensor'), may hold values from -0.1875 to 0.1875
- key_weight: bfloat16 [2, 512, 1024], P(None, 'tensor'), may hold values from -0.1875 to 0.1875
- value_weight: bfloat16 [2, 512, 1024], P(None, 'tensor'), may hold values from -0.1875 to 0.1875
- output_weight: bfloat16 [2, 1024, 1024], P(None, 'tensor'), may hold values from -4 to 4
- mixture_gain: float32 [2, 1024], replicated, may hold values from 0.5 to 1.5
- router_weight: bfloat16 [2, 1024, 32], replicated, may hold values from -0.046875 to 0.046875
- gate_weight: bfloat16 [2, 32, 512, 1024], P(None, 'dp', 'tensor'), may hold values from -0.1875 to 0.1875
- up_weight: bfloat16 [2, 32, 512, 1024], P(None, 'dp', 'tensor'), may hold values from -0.1875 to 0.1875
- down_weight: bfloat16 [2, 32, 512, 1024], P(None, 'dp', 'tensor'), may hold values from -6 to 6
Outputs:
- block_output: float32 [2048, 1024], P('dp')
- input_gradient: float32 [2048, 1024], P('dp')
- attention_gain_gradient: float32 [2, 1024], P(None, 'dp')
- query_gradient: float32 [2, 1024, 1024], P(None, 'dp', 'tensor')
- key_gradient: float32 [2, 512, 1024], P(None, 'tensor', 'dp')
- value_gradient: float32 [2, 512, 1024], P(None, 'tensor', 'dp')
- projection_gradient: float32 [2, 1024, 1024], P(None, 'tensor', 'dp')
- mixture_gain_gradient: float32 [2, 1024], P(None, 'dp')
- router_gradient: float32 [2, 1024, 32], P(None, 'dp')
- gate_gradient: float32 [2, 32, 512, 1024], P(None, 'dp', 'tensor')
- up_gradient: float32 [2, 32, 512, 1024], P(None, 'dp', 'tensor')
- down_gradient: float32 [2, 32, 512, 1024], P(None, 'dp', 'tensor')
Inputs may be any that keep to these rules, and one draw needn't show every extreme that they name: `routes`: each row names 8 different experts; among the rows of one block of 256 rows no expert is named more than 96 times, a bound that some block reaches.
All inputs are finite; a program needn't handle non-finite values.
Results may differ from a plain program's by a relative error of at most 0.02.
Values may be sent and summed in bfloat16 or wider, within the bound.
A program may use at most 256 MiB of HBM per device.

v0:
```python
import jax
import jax.numpy as jnp
from jax import lax
from jax.sharding import PartitionSpec as P

HD = 64
EXPERTS = 32
TOPK = 8
SEQ = 256
CAP = 96


EPSILON = 1e-06
RESIDUAL_SCALE = 0.22
SCORE_SCALE = 0.015625
ROPE_BASE = 10000.0
NEG_LARGE = -1e30


def rotate_half(values):
    middle = values.shape[-1] // 2
    return jnp.concatenate([-values[..., middle:], values[..., :middle]], axis=-1)


def rope_tables(row_count):
    middle = HD // 2
    positions = (jnp.arange(row_count, dtype=jnp.int32) % SEQ).astype(jnp.float32)
    inverse_rate = ROPE_BASE ** (
        -(jnp.arange(middle, dtype=jnp.int32).astype(jnp.float32) * (2.0 / HD))
    )
    angles = positions[:, None] * inverse_rate[None, :]
    cosine = jnp.concatenate([jnp.cos(angles), jnp.cos(angles)], axis=1)[:, None, :]
    sine = jnp.concatenate([jnp.sin(angles), jnp.sin(angles)], axis=1)[:, None, :]
    return (cosine, sine)


def causal_mask():
    counter = jnp.arange(SEQ, dtype=jnp.int32)
    return counter[:, None] >= counter[None, :]


def dot_full(left, right):
    return jnp.dot(left, right, precision=lax.Precision.HIGHEST, preferred_element_type=jnp.float32)


def slot_targets(routes, experts):
    flat_routes = routes.reshape(-1)
    onehot = (flat_routes[:, None] == jnp.arange(experts, dtype=jnp.int32)[None, :]).astype(
        jnp.int32
    )
    before = jnp.cumsum(onehot, axis=0) - onehot
    slot_index = jnp.sum(before * onehot, axis=1)
    return (flat_routes * CAP + slot_index).reshape(routes.shape)


def norm_forward(source, gain):
    inverse_root = lax.rsqrt(jnp.mean(source * source, axis=1, keepdims=True) + EPSILON)
    return (inverse_root, source * inverse_root * gain)


def norm_backward(grad_in, source, inverse_root, gain):
    gain_grad = jnp.sum(grad_in * source * inverse_root, axis=0)
    scaled = grad_in * gain
    inner = jnp.mean(scaled * source, axis=1, keepdims=True)
    return (inverse_root * (scaled - source * inverse_root * inverse_root * inner), gain_grad)


def attend_forward(query, keys, values):
    scores = (
        jnp.einsum("sqkgd,stkd->skgqt", query, keys, preferred_element_type=jnp.float32)
        * SCORE_SCALE
    )
    scores = jnp.where(causal_mask(), scores, NEG_LARGE)
    highest = jnp.max(scores, axis=-1, keepdims=True)
    weights = jnp.exp(scores - highest)
    totals = jnp.sum(weights, axis=-1, keepdims=True)
    log_total = highest + jnp.log(totals)
    probability = (weights / totals).astype(jnp.bfloat16)
    attended = jnp.einsum(
        "skgqt,stkd->sqkgd", probability, values, preferred_element_type=jnp.float32
    )
    return (attended.astype(jnp.bfloat16), log_total)


def attend_backward(query, keys, values, attended, log_total, grad_out):
    scores = (
        jnp.einsum("sqkgd,stkd->skgqt", query, keys, preferred_element_type=jnp.float32)
        * SCORE_SCALE
    )
    scores = jnp.where(causal_mask(), scores, NEG_LARGE)
    probability = jnp.exp(scores - log_total)
    value_grad = jnp.einsum(
        "skgqt,sqkgd->stkd",
        probability.astype(jnp.bfloat16),
        grad_out,
        preferred_element_type=jnp.float32,
    )
    prob_grad = jnp.einsum(
        "sqkgd,stkd->skgqt", grad_out, values, preferred_element_type=jnp.float32
    )
    delta_rows = jnp.sum(grad_out.astype(jnp.float32) * attended.astype(jnp.float32), axis=-1)
    delta_rows = jnp.transpose(delta_rows, (0, 2, 3, 1))[..., None]
    score_grad = (probability * (prob_grad - delta_rows)).astype(jnp.bfloat16)
    query_grad = (
        jnp.einsum("skgqt,stkd->sqkgd", score_grad, keys, preferred_element_type=jnp.float32)
        * SCORE_SCALE
    )
    key_grad = (
        jnp.einsum("skgqt,sqkgd->stkd", score_grad, query, preferred_element_type=jnp.float32)
        * SCORE_SCALE
    )
    return (query_grad, key_grad, value_grad)


def router_backward(weight_grad, router_probs, chosen):
    prob_grad = jnp.sum(chosen * weight_grad[:, :, None], axis=1)
    return router_probs * (prob_grad - jnp.sum(router_probs * prob_grad, axis=1, keepdims=True))


def layer_forward(inputs, params, targets, chosen, cosine, sine):
    (
        attention_gain,
        query_weight,
        key_weight,
        value_weight,
        output_weight,
        mixture_gain,
        router_weight,
        gate_shard,
        up_shard,
        down_shard,
    ) = params
    row_count, width = inputs.shape
    query_heads = query_weight.shape[1] // HD
    key_heads = key_weight.shape[0] // HD
    group_size = query_heads // key_heads
    seq_count = row_count // SEQ
    first_scale, first_normed = norm_forward(inputs, attention_gain)
    first_input = first_normed.astype(jnp.bfloat16)
    query = jnp.dot(first_input, query_weight, preferred_element_type=jnp.float32).reshape(
        row_count, query_heads, HD
    )
    keys = jnp.dot(first_input, key_weight.T, preferred_element_type=jnp.float32).reshape(
        row_count, key_heads, HD
    )
    values = jnp.dot(first_input, value_weight.T, preferred_element_type=jnp.float32).astype(
        jnp.bfloat16
    )
    query = (query * cosine + rotate_half(query) * sine).astype(jnp.bfloat16)
    keys = (keys * cosine + rotate_half(keys) * sine).astype(jnp.bfloat16)
    query_split = query.reshape(seq_count, SEQ, key_heads, group_size, HD)
    key_split = keys.reshape(seq_count, SEQ, key_heads, HD)
    value_split = values.reshape(seq_count, SEQ, key_heads, HD)
    attended, log_total = attend_forward(query_split, key_split, value_split)
    attended_rows = attended.reshape(row_count, query_heads * HD)
    attention_out = lax.psum(
        jnp.dot(attended_rows, output_weight, preferred_element_type=jnp.float32), "tensor"
    )
    middle_state = inputs + RESIDUAL_SCALE * attention_out
    second_scale, second_normed = norm_forward(middle_state, mixture_gain)
    second_input = second_normed.astype(jnp.bfloat16)
    logits = jnp.dot(second_input, router_weight, preferred_element_type=jnp.float32)
    router_probs = jax.nn.softmax(logits, axis=1)
    route_weights = jnp.sum(chosen * router_probs[:, None, :], axis=2)
    flat_targets = targets.reshape(-1)
    dispatched = (
        jnp.zeros((EXPERTS * CAP, width), jnp.bfloat16)
        .at[flat_targets]
        .set(jnp.repeat(second_input, TOPK, axis=0))
        .reshape(EXPERTS, CAP, width)
    )
    received = lax.all_to_all(dispatched, "dp", split_axis=0, concat_axis=1, tiled=True)
    gate_pre = jnp.einsum("ecd,efd->ecf", received, gate_shard, preferred_element_type=jnp.float32)
    up_pre = jnp.einsum("ecd,efd->ecf", received, up_shard, preferred_element_type=jnp.float32)
    activated = (jax.nn.silu(gate_pre) * up_pre).astype(jnp.bfloat16)
    partial_out = jnp.einsum(
        "ecf,efd->ecd", activated, down_shard, preferred_element_type=jnp.float32
    )
    expert_out = (
        lax.all_to_all(
            partial_out.astype(jnp.bfloat16), "dp", split_axis=1, concat_axis=0, tiled=True
        )
        .astype(partial_out.dtype)
        .reshape(EXPERTS * CAP, width)
    )
    picked = expert_out[targets]
    mixture_out = lax.psum(
        jnp.sum(route_weights[:, :, None] * picked, axis=1).astype(jnp.bfloat16), "tensor"
    ).astype(jnp.float32)
    outputs = middle_state + RESIDUAL_SCALE * mixture_out
    saved = (
        first_scale,
        first_input,
        query_split,
        key_split,
        value_split,
        attended,
        log_total,
        middle_state,
        second_scale,
        second_input,
        router_probs,
        route_weights,
        received,
        gate_pre,
        up_pre,
        activated,
        picked,
    )
    return (outputs, saved)


def layer_backward(grad_out, saved, params, targets, chosen, cosine, sine, inputs):
    (
        attention_gain,
        query_weight,
        key_weight,
        value_weight,
        output_weight,
        mixture_gain,
        router_weight,
        gate_shard,
        up_shard,
        down_shard,
    ) = params
    (
        first_scale,
        first_input,
        query_split,
        key_split,
        value_split,
        attended,
        log_total,
        middle_state,
        second_scale,
        second_input,
        router_probs,
        route_weights,
        received,
        gate_pre,
        up_pre,
        activated,
        picked,
    ) = saved
    row_count, width = grad_out.shape
    query_heads = query_weight.shape[1] // HD
    key_heads = key_weight.shape[0] // HD
    mixture_grad = RESIDUAL_SCALE * grad_out
    weight_part = jnp.sum(mixture_grad[:, None, :] * picked, axis=2)
    spread = (
        (route_weights[:, :, None] * mixture_grad[:, None, :])
        .astype(jnp.bfloat16)
        .reshape(row_count * TOPK, width)
    )
    out_grad = (
        jnp.zeros((EXPERTS * CAP, width), jnp.bfloat16)
        .at[targets.reshape(-1)]
        .set(spread)
        .reshape(EXPERTS, CAP, width)
    )
    out_received = lax.all_to_all(out_grad, "dp", split_axis=0, concat_axis=1, tiled=True)
    act_grad = jnp.einsum(
        "ecd,efd->ecf", out_received, down_shard, preferred_element_type=jnp.float32
    )
    down_grad = jnp.einsum(
        "ecf,ecd->efd", activated, out_received, preferred_element_type=jnp.float32
    )
    sigma = jax.nn.sigmoid(gate_pre)
    gate_rows = (act_grad * up_pre * sigma * (1.0 + gate_pre * (1.0 - sigma))).astype(jnp.bfloat16)
    up_rows = (act_grad * gate_pre * sigma).astype(jnp.bfloat16)
    gate_grad = jnp.einsum("ecf,ecd->efd", gate_rows, received, preferred_element_type=jnp.float32)
    up_grad = jnp.einsum("ecf,ecd->efd", up_rows, received, preferred_element_type=jnp.float32)
    dispatch_part = jnp.einsum(
        "ecf,efd->ecd", gate_rows, gate_shard, preferred_element_type=jnp.float32
    ) + jnp.einsum("ecf,efd->ecd", up_rows, up_shard, preferred_element_type=jnp.float32)
    dispatch_grad = (
        lax.all_to_all(
            dispatch_part.astype(jnp.bfloat16), "dp", split_axis=1, concat_axis=0, tiled=True
        )
        .astype(dispatch_part.dtype)
        .reshape(EXPERTS * CAP, width)
    )
    input_part = jnp.sum(dispatch_grad[targets], axis=1)
    router_float = router_weight.astype(jnp.float32)
    weight_grad = lax.psum(weight_part, "tensor")
    logit_grad = router_backward(weight_grad, router_probs, chosen)
    second_grad = lax.psum(input_part.astype(jnp.bfloat16), "tensor").astype(
        jnp.float32
    ) + dot_full(logit_grad, router_float.T)
    router_grad = dot_full(second_input.astype(jnp.float32).T, logit_grad)
    middle_norm_grad, mixture_gain_grad = norm_backward(
        second_grad, middle_state, second_scale, mixture_gain
    )
    middle_grad = grad_out + middle_norm_grad
    attention_grad = (RESIDUAL_SCALE * middle_grad).astype(jnp.bfloat16)
    attended_rows = attended.reshape(row_count, query_heads * HD)
    output_grad = jnp.dot(attended_rows.T, attention_grad, preferred_element_type=jnp.float32)
    attended_grad = jnp.dot(
        attention_grad, output_weight.T, preferred_element_type=jnp.float32
    ).astype(jnp.bfloat16)
    query_grad, key_grad, value_grad = attend_backward(
        query_split,
        key_split,
        value_split,
        attended,
        log_total,
        attended_grad.reshape(attended.shape),
    )
    query_grad = query_grad.reshape(row_count, query_heads, HD)
    query_grad = (
        (query_grad * cosine - rotate_half(query_grad) * sine)
        .astype(jnp.bfloat16)
        .reshape(row_count, query_heads * HD)
    )
    key_grad = key_grad.reshape(row_count, key_heads, HD)
    key_grad = (
        (key_grad * cosine - rotate_half(key_grad) * sine)
        .astype(jnp.bfloat16)
        .reshape(row_count, key_heads * HD)
    )
    value_grad = value_grad.astype(jnp.bfloat16).reshape(row_count, key_heads * HD)
    query_weight_grad = jnp.dot(first_input.T, query_grad, preferred_element_type=jnp.float32)
    key_weight_grad = jnp.dot(key_grad.T, first_input, preferred_element_type=jnp.float32)
    value_weight_grad = jnp.dot(value_grad.T, first_input, preferred_element_type=jnp.float32)
    first_part = (
        jnp.dot(query_grad, query_weight.T, preferred_element_type=jnp.float32)
        + jnp.dot(key_grad, key_weight, preferred_element_type=jnp.float32)
        + jnp.dot(value_grad, value_weight, preferred_element_type=jnp.float32)
    )
    first_grad = lax.psum(first_part.astype(jnp.bfloat16), "tensor").astype(jnp.float32)
    input_norm_grad, attention_gain_grad = norm_backward(
        first_grad, inputs, first_scale, attention_gain
    )
    input_grad = middle_grad + input_norm_grad
    dense = (
        attention_gain_grad,
        query_weight_grad,
        key_weight_grad,
        value_weight_grad,
        output_grad,
        mixture_gain_grad,
        router_grad,
    )
    return (input_grad, dense, (gate_grad, up_grad, down_grad))


def shards(
    hidden_states,
    output_cotangent,
    routes,
    attention_gain,
    query_weight,
    key_weight,
    value_weight,
    output_weight,
    mixture_gain,
    router_weight,
    gate_weight,
    up_weight,
    down_weight,
):
    params_all = (
        attention_gain,
        query_weight,
        key_weight,
        value_weight,
        output_weight,
        mixture_gain,
        router_weight,
        gate_weight,
        up_weight,
        down_weight,
    )
    row_count = hidden_states.shape[0]
    layer_count = query_weight.shape[0]
    cosine, sine = rope_tables(row_count)
    targets = slot_targets(routes, EXPERTS)
    chosen = (routes[:, :, None] == jnp.arange(EXPERTS, dtype=jnp.int32)[None, None, :]).astype(
        jnp.float32
    )
    current = hidden_states
    kept = []
    for layer_index in range(layer_count):
        layer_params = tuple((weight[layer_index] for weight in params_all))
        layer_input = current
        current, saved = layer_forward(current, layer_params, targets, chosen, cosine, sine)
        kept.append((saved, layer_input))
    grad_now = output_cotangent
    dense_layers = [None] * layer_count
    expert_layers = [None] * layer_count
    for layer_index in reversed(range(layer_count)):
        layer_params = tuple((weight[layer_index] for weight in params_all))
        grad_now, dense, expert_grads = layer_backward(
            grad_now,
            kept[layer_index][0],
            layer_params,
            targets,
            chosen,
            cosine,
            sine,
            kept[layer_index][1],
        )
        dense_layers[layer_index] = dense
        expert_layers[layer_index] = expert_grads
    stacked = tuple(
        (jnp.stack([entry[position] for entry in dense_layers]) for position in range(7))
    )
    stacked = (
        lax.psum_scatter(
            stacked[0].astype(jnp.bfloat16), "dp", scatter_dimension=1, tiled=True
        ).astype(jnp.float32),
        lax.psum_scatter(
            stacked[1].astype(jnp.bfloat16), "dp", scatter_dimension=1, tiled=True
        ).astype(jnp.float32),
        lax.psum_scatter(
            stacked[2].astype(jnp.bfloat16), "dp", scatter_dimension=2, tiled=True
        ).astype(jnp.float32),
        lax.psum_scatter(
            stacked[3].astype(jnp.bfloat16), "dp", scatter_dimension=2, tiled=True
        ).astype(jnp.float32),
        lax.psum_scatter(
            stacked[4].astype(jnp.bfloat16), "dp", scatter_dimension=2, tiled=True
        ).astype(jnp.float32),
        lax.psum_scatter(
            stacked[5].astype(jnp.bfloat16), "dp", scatter_dimension=1, tiled=True
        ).astype(jnp.float32),
        lax.psum_scatter(
            stacked[6].astype(jnp.bfloat16), "dp", scatter_dimension=1, tiled=True
        ).astype(jnp.float32),
    )
    experts_stacked = tuple(
        (jnp.stack([entry[position] for entry in expert_layers]) for position in range(3))
    )
    return (
        current,
        grad_now,
        stacked[0],
        stacked[1],
        stacked[2],
        stacked[3],
        stacked[4],
        stacked[5],
        stacked[6],
        experts_stacked[0],
        experts_stacked[1],
        experts_stacked[2],
    )


def solution(mesh):
    placed = (
        P("dp", None),
        P("dp", None),
        P("dp", None),
        P(),
        P(None, None, "tensor"),
        P(None, "tensor", None),
        P(None, "tensor", None),
        P(None, "tensor", None),
        P(),
        P(),
        P(None, "dp", "tensor", None),
        P(None, "dp", "tensor", None),
        P(None, "dp", "tensor", None),
    )
    return jax.shard_map(
        shards,
        mesh=mesh,
        in_specs=placed,
        out_specs=(
            P("dp", None),
            P("dp", None),
            P(None, "dp"),
            P(None, "dp", "tensor"),
            P(None, "tensor", "dp"),
            P(None, "tensor", "dp"),
            P(None, "tensor", "dp"),
            P(None, "dp"),
            P(None, "dp", None),
            P(None, "dp", "tensor", None),
            P(None, "dp", "tensor", None),
            P(None, "dp", "tensor", None),
        ),
        check_vma=False,
    )
```

profile of v0, /device:TPU:0, one launch (start us, length us, event | category | flops | bytes accessed | tf_op | source)
XLA Modules:
  0.0 1461.2 jit_solution(3478899674572647323)
XLA Ops:
  22.6 9.1 reduce-window.6
  32.9 44.1 %all-reduce.9.cloned.1.call-done = f32[256,1024]{1,0:T(8,128)} async-done(((f32[256,1024]{1,0:T(8,128)}), f32[256,1024]{1,0:T(8,128)}) %all-reduce.9.cloned.1.call-update) | async-done | bytes 1048592 | tf_op jit(solution)/shard_map/psum | solution.py:156
  78.7 13.6 scatter_custom_fusion
  92.3 75.7 %all_to_all.108 = bf16[32,96,1024]{2,1,0:T(8,128)(2,1)S(1)} all-to-all(bf16[32,96,1024]{2,1,0:T(8,128)(2,1)} %bitcast.564), channel_id=1, replica_groups=mesh['dp'=8,'tensor'=4] {'dp'}, dimensions={0} | all-to-all | bytes 12582912 | tf_op jit(solution)/shard_map/all_to_all | solution.py:172
  176.6 4.5 convolution_convert_fusion.1
  181.1 10.3 copy.162
  191.4 4.9 all-to-all-start.1
  197.3 70.6 %all-to-all-done.1 = bf16[4,768,1024]{2,0,1:T(4,128)(2,1)} async-done(((bf16[4,768,1024]{2,0,1:T(4,128)(2,1)}), bf16[4,768,1024]{2,0,1:T(4,128)(2,1)}, u32[]{:S(2)}, u32[]{:S(2)}) %all-to-all-start.1) | async-done | bytes 6291488 | tf_op jit(solution)/shard_map/all_to_all | solution.py:180
  267.9 9.7 copy.163
  277.6 16.3 %gather_fusion = f32[2048,1024]{1,0:T(8,128)} fusion(f32[3072,1024]{1,0:T(8,128)} %bitcast.540, s32[2048]{0:T(1024)S(1)} %broadcast_clamp_fusion), kind=kCustom, calls=%fused_computation | custom fusion | bytes 16785408 | tf_op jit(solution)/shard_map/gather | solution.py:186
  293.9 6.7 fusion.5
  301.9 34.8 %all-reduce.11.cloned.1.call-done = bf16[256,1024]{1,0:T(8,128)(2,1)} async-done(((bf16[256,1024]{1,0:T(8,128)(2,1)}), bf16[256,1024]{1,0:T(8,128)(2,1)}) %all-reduce.11.cloned.1.call-update) | async-done | bytes 524304 | tf_op jit(solution)/shard_map/psum | solution.py:187
  345.4 51.8 %all-reduce.13.cloned.1.call-done = f32[256,1024]{1,0:T(8,128)} async-done(((f32[256,1024]{1,0:T(8,128)}), f32[256,1024]{1,0:T(8,128)}) %all-reduce.13.cloned.1.call-update) | async-done | bytes 1048592 | tf_op jit(solution)/shard_map/psum | solution.py:156
  399.8 14.0 scatter_custom_fusion.1
  413.8 5.1 all-to-all-start.2
  424.0 14.6 scatter_custom_fusion.2
  438.6 51.9 %all-to-all-done.2 = bf16[32,96,1024]{2,1,0:T(8,128)(2,1)} async-done(((bf16[32,96,1024]{2,1,0:T(8,128)(2,1)}), bf16[32,96,1024]{2,1,0:T(8,128)(2,1)}, u32[]{:S(2)}, u32[]{:S(2)}) %all-to-all-start.2) | async-done | bytes 6291488 | tf_op jit(solution)/shard_map/all_to_all | solution.py:172
  490.5 5.2 all-to-all-start.4
  495.7 3.6 copy.167
  505.6 61.2 %all-to-all-done.4 = bf16[32,96,1024]{2,1,0:T(8,128)(2,1)} async-done(((bf16[32,96,1024]{2,1,0:T(8,128)(2,1)}), bf16[32,96,1024]{2,1,0:T(8,128)(2,1)}, u32[]{:S(2)}, u32[]{:S(2)}) %all-to-all-start.4) | async-done | bytes 6291488 | tf_op jit(solution)/shard_map/all_to_all | solution.py:261
  566.8 3.7 copy.171
  575.6 4.5 convolution_convert_fusion
  580.1 10.5 copy.168
  590.6 4.8 all-to-all-start.3
  598.8 4.5 add_convert_fusion.1
  603.3 10.2 copy.172
  613.5 53.4 %all-to-all-done.3 = bf16[4,768,1024]{2,0,1:T(4,128)(2,1)} async-done(((bf16[4,768,1024]{2,0,1:T(4,128)(2,1)}), bf16[4,768,1024]{2,0,1:T(4,128)(2,1)}, u32[]{:S(2)}, u32[]{:S(2)}) %all-to-all-start.3) | async-done | bytes 6291488 | tf_op jit(solution)/shard_map/all_to_all | solution.py:180
  666.9 4.7 all-to-all-start.5
  671.9 9.7 copy.169
  681.6 16.4 %gather_fusion.1 = f32[2048,1024]{1,0:T(8,128)} fusion(f32[3072,1024]{1,0:T(8,128)} %bitcast.541, s32[2048]{0:T(1024)S(1)} %broadcast_clamp_fusion), kind=kCustom, calls=%fused_computation.1 | custom fusion | bytes 16785408 | tf_op jit(solution)/shard_map/gather | solution.py:186
  698.0 45.2 %all-to-all-done.5 = bf16[4,768,1024]{2,0,1:T(4,128)(2,1)} async-done(((bf16[4,768,1024]{2,0,1:T(4,128)(2,1)}), bf16[4,768,1024]{2,0,1:T(4,128)(2,1)}, u32[]{:S(2)}, u32[]{:S(2)}) %all-to-all-start.5) | async-done | bytes 6291488 | tf_op jit(solution)/shard_map/all_to_all | solution.py:277
  743.2 9.7 copy.173
  752.9 16.3 %gather_fusion.2 = f32[2048,1024]{1,0:T(8,128)} fusion(f32[3072,1024]{1,0:T(8,128)} %bitcast.542, s32[2048]{0:T(1024)S(1)} %broadcast_clamp_fusion), kind=kCustom, calls=%fused_computation.2 | custom fusion | bytes 16785408 | tf_op jit(solution)/shard_map/gather | solution.py:283
  769.2 6.3 bitcast_reduce_fusion.1
  775.5 6.4 fusion.2
  782.0 20.7 %psum.75 = f32[256,8]{1,0:T(8,128)S(1)} all-reduce(f32[256,8]{1,0:T(8,128)S(1)} %get-tuple-element.12), channel_id=1, replica_groups=mesh['dp'=8,'tensor'=4] {'tensor'}, use_global_device_ids=true, to_apply=%region_29.30 | all-reduce | flops 2048 | bytes 16384 | tf_op jit(solution)/shard_map/psum | solution.py:285
  803.5 9.2 all-reduce.15.cloned.1.call-done
  823.0 38.5 %all-reduce.17.cloned.1.call-done = bf16[256,1024]{1,0:T(8,128)(2,1)} async-done(((bf16[256,1024]{1,0:T(8,128)(2,1)}), bf16[256,1024]{1,0:T(8,128)(2,1)}) %all-reduce.17.cloned.1.call-update) | async-done | bytes 524304 | tf_op jit(solution)/shard_map/psum | solution.py:330
  866.3 14.6 scatter_custom_fusion.3
  880.9 75.4 %all_to_all.109 = bf16[32,96,1024]{2,1,0:T(8,128)(2,1)S(1)} all-to-all(bf16[32,96,1024]{2,1,0:T(8,128)(2,1)} %bitcast.561), channel_id=1, replica_groups=mesh['dp'=8,'tensor'=4] {'dp'}, dimensions={0} | all-to-all | bytes 12582912 | tf_op jit(solution)/shard_map/all_to_all | solution.py:261
  957.7 6.0 multiply_convert_fusion
  965.6 5.8 add_convert_fusion
  971.3 10.3 copy.180
  981.6 4.9 all-to-all-start.7
  987.4 70.7 %all-to-all-done.7 = bf16[4,768,1024]{2,0,1:T(4,128)(2,1)} async-done(((bf16[4,768,1024]{2,0,1:T(4,128)(2,1)}), bf16[4,768,1024]{2,0,1:T(4,128)(2,1)}, u32[]{:S(2)}, u32[]{:S(2)}) %all-to-all-start.7) | async-done | bytes 6291488 | tf_op jit(solution)/shard_map/all_to_all | solution.py:277
  1058.1 9.7 copy.181
  1067.8 16.4 %gather_fusion.3 = f32[2048,1024]{1,0:T(8,128)} fusion(f32[3072,1024]{1,0:T(8,128)} %bitcast.539, s32[2048]{0:T(1024)S(1)} %broadcast_clamp_fusion), kind=kCustom, calls=%fused_computation.3 | custom fusion | bytes 16785408 | tf_op jit(solution)/shard_map/gather | solution.py:283
  1084.2 6.2 bitcast_reduce_fusion
  1090.5 5.2 fusion.4
  1095.7 21.5 %psum.78 = f32[256,8]{1,0:T(8,128)} all-reduce(f32[256,8]{1,0:T(8,128)} %fusion.4), channel_id=1, replica_groups=mesh['dp'=8,'tensor'=4] {'tensor'}, use_global_device_ids=true, to_apply=%region_40.41 | all-reduce | flops 2048 | bytes 16384 | tf_op jit(solution)/shard_map/psum | solution.py:285
  1120.9 7.2 all-reduce.19.cloned.1.call-done
  1157.2 5.5 convolution_bitcast_fusion
  1164.9 5.6 convolution_bitcast_fusion.2
  1171.9 18.8 %all-reduce.21.cloned.1.call-done = (bf16[256,1024]{1,0:T(8,128)(2,1)}, bf16[256,1024]{1,0:T(8,128)(2,1)}) async-done(((bf16[256,1024]{1,0:T(8,128)(2,1)}, bf16[256,1024]{1,0:T(8,128)(2,1)}), (bf16[256,1024]{1,0:T(8,128)(2,1)}, bf16[256,1024]{1,0:T(8,128)(2,1)})) %all-reduce.21.cloned.1.call-update) | async-done | bytes 1048592 | tf_op jit(solution)/shard_map/psum | solution.py:187
  1197.0 5.6 convolution_bitcast_fusion.4
  1202.6 24.1 %reduce-scatter.32.cloned.1.call-done = bf16[128,64]{1,0:T(8,128)(2,1)} async-done(((bf16[1024,64]{1,0:T(8,128)(2,1)}), bf16[128,64]{1,0:T(8,128)(2,1)}) %reduce-scatter.32.cloned.1.call-update) | async-done | bytes 16400
  1228.3 4.2 convolution_bitcast_fusion.1
  1239.3 5.0 pad_maximum_fusion
  1248.3 15.2 %reduce-scatter.30.cloned.1.call-done = bf16[128,2]{1,0:T(8,128)(2,1)} async-done(((bf16[1024,2]{1,0:T(8,128)(2,1)}), bf16[128,2]{1,0:T(8,128)(2,1)}) %reduce-scatter.30.cloned.1.call-update) | async-done | bytes 528
  1264.9 35.7 %reduce-scatter.26.cloned.1.call-done = bf16[128,256]{1,0:T(8,128)(2,1)} async-done(((bf16[1024,256]{1,0:T(8,128)(2,1)}), bf16[128,256]{1,0:T(8,128)(2,1)}) %reduce-scatter.26.cloned.1.call-update) | async-done | bytes 65552
  1302.2 35.6 %reduce-scatter.24.cloned.1.call-done = bf16[128,256]{1,0:T(8,128)(2,1)} async-done(((bf16[1024,256]{1,0:T(8,128)(2,1)}), bf16[128,256]{1,0:T(8,128)(2,1)}) %reduce-scatter.24.cloned.1.call-update) | async-done | bytes 65552
  1344.0 30.4 %reduce-scatter.22.cloned.1.call-done = bf16[128,2]{1,0:T(8,128)(2,1)} async-done(((bf16[1024,2]{1,0:T(8,128)(2,1)}), bf16[128,2]{1,0:T(8,128)(2,1)}) %reduce-scatter.22.cloned.1.call-update) | async-done | bytes 528
  1375.8 37.8 %reduce-scatter.28.cloned.1.call-done = bf16[128,512]{1,0:T(8,128)(2,1)} async-done(((bf16[1024,512]{1,0:T(8,128)(2,1)}), bf16[128,512]{1,0:T(8,128)(2,1)}) %reduce-scatter.28.cloned.1.call-update) | async-done | bytes 131088
  1415.4 37.2 %reduce-scatter.20.cloned.1.call-done = bf16[2,128,256]{2,1,0:T(8,128)(2,1)} async-done(((bf16[2,1024,256]{2,1,0:T(8,128)(2,1)}), bf16[2,128,256]{2,1,0:T(8,128)(2,1)}) %reduce-scatter.20.cloned.1.call-update) | async-done | bytes 131088 | tf_op jit(solution)/shard_map/reduce_scatter | solution.py:412
  (468 shorter events, 148.0 us)
Async XLA Ops:
  7.2 8.6 copy-start.31
  7.2 69.9 %all-reduce.9.cloned.1.call-start = ((), (), s32[]{:S(2)}) async-start(), calls=%async_computation.15 | async-start | bytes 2097152 | tf_op jit(solution)/shard_map/psum | solution.py:156
  7.3 12.2 copy-start.66
  12.7 8.2 copy-start.9
  18.1 323.4 %copy-start.37 = (f32[256,64]{0,1:T(8,128)}, f32[256,64]{0,1:T(8,128)S(1)}, u32[]{:S(2)}) copy-start(f32[256,64]{0,1:T(8,128)S(1)} %get-tuple-element.74) | copy-start | bytes 196612
  19.1 13.7 copy-start.54
  19.1 13.8 copy-start.114
  19.1 58.0 %copy-start.2 = (f32[256,1024]{1,0:T(8,128)S(1)}, f32[256,1024]{1,0:T(8,128)}, u32[]{:S(2)}) copy-start(f32[256,1024]{1,0:T(8,128)} %param.13) | copy-start | bytes 3145732
  19.5 59.0 %copy-start.93 = (f32[2,2,256]{2,1,0:T(2,128)}, f32[2,2,256]{2,1,0:T(2,128)S(1)}, u32[]{:S(2)}) copy-start(f32[2,2,256]{2,1,0:T(2,128)S(1)} %get-tuple-element.81) | copy-start | bytes 12292
  20.9 12.0 copy-start.56
  32.9 135.1 %copy-start.91 = (f32[1,1024]{1,0:T(1,128)}, f32[1,1024]{1,0:T(1,128)S(1)}, u32[]{:S(2)}) copy-start(f32[1,1024]{1,0:T(1,128)S(1)} %get-tuple-element.76) | copy-start | bytes 12292
  32.9 135.0 %copy-start.113 = (s32[2048,1]{0,1:T(1,128)}, s32[2048,1]{0,1:T(1,128)S(1)}, u32[]{:S(2)}) copy-start(s32[2048,1]{0,1:T(1,128)S(1)} %compare_select_fusion.1) | copy-start | bytes 24580
  78.5 89.4 %copy-start.97 = (f32[256]{0:T(256)}, f32[256]{0:T(256)S(1)}, u32[]{:S(2)}) copy-start(f32[256]{0:T(256)S(1)} %add_rsqrt_fusion.2) | copy-start | bytes 3076
  78.7 118.0 %copy-start.25 = (bf16[256,1024]{1,0:T(8,128)(2,1)}, bf16[256,1024]{1,0:T(8,128)(2,1)S(1)}, u32[]{:S(2)}) copy-start(bf16[256,1024]{1,0:T(8,128)(2,1)S(1)} %multiply_convert_fusion.10) | copy-start | bytes 1572868
  191.4 76.5 %all-to-all-start.1 = ((bf16[4,768,1024]{2,0,1:T(4,128)(2,1)}), bf16[4,768,1024]{2,0,1:T(4,128)(2,1)}, u32[]{:S(2)}, u32[]{:S(2)}) async-start(bf16[4,768,1024]{2,0,1:T(4,128)(2,1)} %copy.162), calls=%async_computation.1 | async-start | bytes 12582912 | tf_op jit(solution)/shard_map/all_to_all | solution.py:180
  196.3 140.4 %all-reduce.11.cloned.1.call-start = ((), (), s32[]{:S(2)}) async-start(), calls=%async_computation.16 | async-start | bytes 1048576 | tf_op jit(solution)/shard_map/psum | solution.py:187
  197.0 80.6 %copy-start.75 = (f32[256,32]{0,1:T(8,128)}, f32[256,32]{0,1:T(8,128)S(1)}, u32[]{:S(2)}) copy-start(f32[256,32]{0,1:T(8,128)S(1)} %get-tuple-element.86) | copy-start | bytes 98308
  197.0 80.6 %copy-start.98 = (f32[256]{0:T(256)}, f32[256]{0:T(256)S(1)}, u32[]{:S(2)}) copy-start(f32[256]{0:T(256)S(1)} %get-tuple-element.85) | copy-start | bytes 3076
  197.0 80.6 %copy-start.108 = (f32[256]{0:T(256)}, f32[256]{0:T(256)S(1)}, u32[]{:S(2)}) copy-start(f32[256]{0:T(256)S(1)} %fusion.185) | copy-start | bytes 3076
  197.1 80.5 %copy-start.69 = (f32[256,32]{0,1:T(8,128)}, f32[256,32]{0,1:T(8,128)S(1)}, u32[]{:S(2)}) copy-start(f32[256,32]{0,1:T(8,128)S(1)} %fusion.184) | copy-start | bytes 98308
  293.9 47.3 %copy-start.61 = (bf16[1,128,1024]{2,1,0:T(8,128)(2,1)S(1)}, bf16[1,128,1024]{2,1,0:T(8,128)(2,1)}, u32[]{:S(2)}) copy-start(bf16[1,128,1024]{2,1,0:T(8,128)(2,1)} %get-tuple-element.35) | copy-start | bytes 786436
  300.6 96.7 %all-reduce.13.cloned.1.call-start = ((), (), s32[]{:S(2)}) async-start(), calls=%async_computation.17 | async-start | bytes 2097152 | tf_op jit(solution)/shard_map/psum | solution.py:156
  338.0 525.5 %copy-start.96 = (f32[256]{0:T(256)}, f32[256]{0:T(256)S(1)}, u32[]{:S(2)}) copy-start(f32[256]{0:T(256)S(1)} %add_rsqrt_fusion.1) | copy-start | bytes 3076
  341.1 56.2 %copy-start.15 = (bf16[256,1024]{1,0:T(8,128)(2,1)S(1)}, bf16[256,1024]{1,0:T(8,128)(2,1)}, u32[]{:S(2)}) copy-start(bf16[256,1024]{1,0:T(8,128)(2,1)} %all-reduce.11.cloned.1.call-done) | copy-start | bytes 1572868
  344.1 473.5 %copy-start.59 = (bf16[2,64,2,256]{3,1,2,0:T(8,128)(2,1)}, bf16[2,64,2,256]{3,1,2,0:T(8,128)(2,1)S(1)}, u32[]{:S(2)}) copy-start(bf16[2,64,2,256]{3,1,2,0:T(8,128)(2,1)S(1)} %convolution_convert_fusion.12) | copy-start | bytes 393220
  413.8 7.5 copy-start.74
  413.8 76.7 %all-to-all-start.2 = ((bf16[32,96,1024]{2,1,0:T(8,128)(2,1)}), bf16[32,96,1024]{2,1,0:T(8,128)(2,1)}, u32[]{:S(2)}, u32[]{:S(2)}) async-start(bf16[32,96,1024]{2,1,0:T(8,128)(2,1)} %bitcast.559), calls=%async_computation.2 | async-start | bytes 12582912 | tf_op jit(solution)/shard_map/all_to_all | solution.py:172
  423.7 389.0 %copy-start.70 = (f32[256,32]{0,1:T(8,128)}, f32[256,32]{0,1:T(8,128)S(1)}, u32[]{:S(2)}) copy-start(f32[256,32]{0,1:T(8,128)S(1)} %fusion.186) | copy-start | bytes 98308
  490.5 76.3 %all-to-all-start.4 = ((bf16[32,96,1024]{2,1,0:T(8,128)(2,1)}), bf16[32,96,1024]{2,1,0:T(8,128)(2,1)}, u32[]{:S(2)}, u32[]{:S(2)}) async-start(bf16[32,96,1024]{2,1,0:T(8,128)(2,1)} %bitcast.560), calls=%async_computation.4 | async-start | bytes 12582912 | tf_op jit(solution)/shard_map/all_to_all | solution.py:261
  590.6 76.3 %all-to-all-start.3 = ((bf16[4,768,1024]{2,0,1:T(4,128)(2,1)}), bf16[4,768,1024]{2,0,1:T(4,128)(2,1)}, u32[]{:S(2)}, u32[]{:S(2)}) async-start(bf16[4,768,1024]{2,0,1:T(4,128)(2,1)} %copy.168), calls=%async_computation.3 | async-start | bytes 12582912 | tf_op jit(solution)/shard_map/all_to_all | solution.py:180
  666.9 76.3 %all-to-all-start.5 = ((bf16[4,768,1024]{2,0,1:T(4,128)(2,1)}), bf16[4,768,1024]{2,0,1:T(4,128)(2,1)}, u32[]{:S(2)}, u32[]{:S(2)}) async-start(bf16[4,768,1024]{2,0,1:T(4,128)(2,1)} %copy.172), calls=%async_computation.5 | async-start | bytes 12582912 | tf_op jit(solution)/shard_map/all_to_all | solution.py:277
  671.7 141.1 %all-reduce.15.cloned.1.call-start = ((), (), s32[]{:S(2)}) async-start(), calls=%async_computation.18 | async-start | bytes 1048576 | tf_op jit(solution)/shard_map/psum | solution.py:287
  775.5 27.3 %copy-start.100 = (f32[256]{0:T(256)S(1)}, f32[256]{0:T(256)}, u32[]{:S(2)}) copy-start(f32[256]{0:T(256)} %copy-done.99) | copy-start | bytes 3076
  775.5 86.0 %all-reduce.17.cloned.1.call-start = ((), (), s32[]{:S(2)}) async-start(), calls=%async_computation.19 | async-start | bytes 1048576 | tf_op jit(solution)/shard_map/psum | solution.py:330
  802.7 15.3 %copy-start.87 = (bf16[256,128]{0,1:T(8,128)(2,1)S(1)}, bf16[256,128]{0,1:T(8,128)(2,1)}, u32[]{:S(2)}) copy-start(bf16[256,128]{0,1:T(8,128)(2,1)} %copy-done.86) | copy-start | bytes 196612
  802.8 10.0 copy-start.71
  803.5 15.1 %copy-start.106 = (f32[256]{0:T(256)}, f32[256]{0:T(256)S(1)}, u32[]{:S(2)}) copy-start(f32[256]{0:T(256)S(1)} %multiply_reduce_fusion.9) | copy-start | bytes 3076
  863.6 92.7 %copy-start.110 = (f32[256]{0:T(256)}, f32[256]{0:T(256)S(1)}, u32[]{:S(2)}) copy-start(f32[256]{0:T(256)S(1)} %broadcast_multiply_fusion.12) | copy-start | bytes 3076
  981.6 76.5 %all-to-all-start.7 = ((bf16[4,768,1024]{2,0,1:T(4,128)(2,1)}), bf16[4,768,1024]{2,0,1:T(4,128)(2,1)}, u32[]{:S(2)}, u32[]{:S(2)}) async-start(bf16[4,768,1024]{2,0,1:T(4,128)(2,1)} %copy.180), calls=%async_computation.7 | async-start | bytes 12582912 | tf_op jit(solution)/shard_map/all_to_all | solution.py:277
  986.5 141.6 %all-reduce.19.cloned.1.call-start = ((), (), s32[]{:S(2)}) async-start(), calls=%async_computation.20 | async-start | bytes 1048576 | tf_op jit(solution)/shard_map/psum | solution.py:287
  1090.4 37.7 %copy-start.92 = (f32[1,1024]{1,0:T(1,128)S(1)}, f32[1,1024]{1,0:T(1,128)}, u32[]{:S(2)}) copy-start(f32[1,1024]{1,0:T(1,128)} %copy-done.91) | copy-start | bytes 12292
  1090.4 40.5 %copy-start.6 = (f32[256,1024]{1,0:T(8,128)S(1)}, f32[256,1024]{1,0:T(8,128)}, u32[]{:S(2)}) copy-start(f32[256,1024]{1,0:T(8,128)} %copy-done.5) | copy-start | bytes 3145732
  1090.4 100.3 %all-reduce.21.cloned.1.call-start = ((), (), s32[]{:S(2)}) async-start(), calls=%async_computation.28 | async-start | bytes 2097152 | tf_op jit(solution)/shard_map/psum | solution.py:187
  1120.1 13.3 copy-start.95
  1136.1 12.1 copy-start.112
  1136.1 13.0 copy-start.10
  1138.8 87.9 %reduce-scatter.32.cloned.1.call-start = ((), (), s32[]{:S(2)}) async-start(), calls=%async_computation.27 | async-start | bytes 294912
  1148.1 115.4 %reduce-scatter.30.cloned.1.call-start = ((), (), s32[]{:S(2)}) async-start(), calls=%async_computation.26 | async-start | bytes 294912
  1150.9 149.7 %reduce-scatter.26.cloned.1.call-start = ((), (), s32[]{:S(2)}) async-start(), calls=%async_computation.24 | async-start | bytes 589824
  1152.8 9.9 copy-start.38
  1156.8 181.0 %reduce-scatter.24.cloned.1.call-start = ((), (), s32[]{:S(2)}) async-start(), calls=%async_computation.23 | async-start | bytes 589824
  1163.8 7.8 copy-start.115
  1164.7 26.0 %copy-start.3 = (f32[256,1024]{1,0:T(8,128)S(1)}, f32[256,1024]{1,0:T(8,128)}, u32[]{:S(2)}) copy-start(f32[256,1024]{1,0:T(8,128)} %param.13) | copy-start | bytes 3145732
  1164.8 25.9 %copy-start.89 = (f32[1,1024]{1,0:T(1,128)S(1)}, f32[1,1024]{1,0:T(1,128)}, u32[]{:S(2)}) copy-start(f32[1,1024]{1,0:T(1,128)} %copy-done.88) | copy-start | bytes 12292
  1164.8 25.9 %copy-start.104 = (f32[256]{0:T(256)S(1)}, f32[256]{0:T(256)}, u32[]{:S(2)}) copy-start(f32[256]{0:T(256)} %copy-done.103) | copy-start | bytes 3076
  1164.8 209.6 %reduce-scatter.22.cloned.1.call-start = ((), (), s32[]{:S(2)}) async-start(), calls=%async_computation.22 | async-start | bytes 294912
  1193.6 220.0 %reduce-scatter.28.cloned.1.call-start = ((), (), s32[]{:S(2)}) async-start(), calls=%async_computation.25 | async-start | bytes 1179648
  1197.0 255.7 %reduce-scatter.20.cloned.1.call-start = ((), (), s32[]{:S(2)}) async-start(), calls=%async_computation.21 | async-start | bytes 1179648 | tf_op jit(solution)/shard_map/reduce_scatter | solution.py:412
  1197.0 37.8 %slice-start = ((s8[6291456]{0:T(1024)(128)(4,1)}), s8[2097152]{0:T(1024)(128)(4,1)S(1)}, s32[]{:S(2)}) async-start(s8[6291456]{0:T(1024)(128)(4,1)} %bitcast.545), calls=%async_computation.29 | async-start | bytes 4194304
  1245.9 93.6 %copy-start.116 = (f32[256]{0:T(256)S(1)}, f32[256]{0:T(256)}, u32[]{:S(2)}) copy-start(f32[256]{0:T(256)} %get-tuple-element.21) | copy-start | bytes 3076
  1245.9 95.7 %copy-start.4 = (f32[256,1024]{1,0:T(8,128)S(1)}, f32[256,1024]{1,0:T(8,128)}, u32[]{:S(2)}) copy-start(f32[256,1024]{1,0:T(8,128)} %param.13) | copy-start | bytes 3145732
  1245.9 95.7 %copy-start.22 = (f32[256,1024]{1,0:T(8,128)S(1)}, f32[256,1024]{1,0:T(8,128)}, u32[]{:S(2)}) copy-start(f32[256,1024]{1,0:T(8,128)} %copy-done.20) | copy-start | bytes 3145732
  1245.9 95.7 %copy-start.90 = (f32[1,1024]{1,0:T(1,128)S(1)}, f32[1,1024]{1,0:T(1,128)}, u32[]{:S(2)}) copy-start(f32[1,1024]{1,0:T(1,128)} %copy-done.88) | copy-start | bytes 12292
  1245.9 95.7 %copy-start.105 = (f32[256]{0:T(256)S(1)}, f32[256]{0:T(256)}, u32[]{:S(2)}) copy-start(f32[256]{0:T(256)} %copy-done.103) | copy-start | bytes 3076
  (81 other events, 324.4 us)
Sparse Core Ops, SparseCore 0:
  22.4 54.6 all-reduce.8
  300.7 35.9 all-reduce.10
  345.6 51.6 all-reduce.12
  775.6 37.0 all-reduce.14
  823.0 38.4 all-reduce.16
  1090.5 37.5 all-reduce.18
  1138.9 51.7 all-reduce.20
  1193.7 32.9 reduce-scatter.31
  1229.7 33.7 reduce-scatter.29
  1266.4 34.1 reduce-scatter.25
  1303.6 34.1 reduce-scatter.23
  1340.7 33.6 reduce-scatter.21
  1377.6 35.9 reduce-scatter.27
  1416.6 35.9 reduce-scatter.19
where the time goes:
time: 1470 us; the launch traced here: 1460 us
  waiting for transfers between devices  774 us (53%)
  local copies, waits for them, and re-layouts  218 us (15%)
  blocking collectives  193 us (13%)
  other arithmetic  127 us (9%)
  matrix products  102 us (7%)
  starting transfers between devices  31 us (2%)
  between operations  16.4 us (1%)
    unnamed x20, waiting for transfers between devices  179 us
    all_to_all x2, waiting for transfers between devices, layer_forward(): lax.all_to_all(partial_out.astype(jnp.bfloat16), 'dp', split_axis=1, conc...  124 us
    all_to_all x2, waiting for transfers between devices, layer_backward(): lax.all_to_all(dispatch_part.astype(jnp.bfloat16), 'dp', split_axis=1, co...  116 us
    psum x2, waiting for transfers between devices, layer_forward(): lax.psum(jnp.dot(attended_rows, output_weight, preferred_element_type=jnp...  96 us
    all_to_all x1, blocking collectives, layer_forward(): lax.all_to_all(dispatched, 'dp', split_axis=0, concat_axis=1, tiled=True)  75.7 us
    all_to_all x1, blocking collectives, layer_backward(): lax.all_to_all(out_grad, 'dp', split_axis=0, concat_axis=1, tiled=True)  75.4 us
    all_to_all x1, waiting for transfers between devices, layer_backward(): lax.all_to_all(out_grad, 'dp', split_axis=0, concat_axis=1, tiled=True)  61.2 us
    psum x2, waiting for transfers between devices, layer_forward(): lax.psum(jnp.sum(route_weights[:, :, None] * picked, axis=1).astype(jnp.b...  53.6 us
  transfers between devices with their start and end apart: 20, of which 20 were waited for; matrix products, arithmetic and copies ran while one was open for 12% of the time, Pallas kernels for 0%

commit v1 on v0

v1 whole, which is shorter than its diff:
```python
import functools

import jax
import jax.numpy as jnp
from jax import lax
from jax.experimental import pallas as pl
from jax.experimental.pallas import tpu as pltpu
from jax.sharding import PartitionSpec as P

HD = 64
EXPERTS = 32
SEQ = 256


EPSILON = 1e-06
RESIDUAL_SCALE = 0.22
SCORE_SCALE = 0.015625
ROPE_BASE = 10000.0
NEG_LARGE = -1e30


def rotate_half(values):
    middle = values.shape[-1] // 2
    return jnp.concatenate([-values[..., middle:], values[..., :middle]], axis=-1)


def rope_tables(row_count):
    middle = HD // 2
    positions = (jnp.arange(row_count, dtype=jnp.int32) % SEQ).astype(jnp.float32)
    inverse_rate = ROPE_BASE ** (
        -(jnp.arange(middle, dtype=jnp.int32).astype(jnp.float32) * (2.0 / HD))
    )
    angles = positions[:, None] * inverse_rate[None, :]
    cosine = jnp.concatenate([jnp.cos(angles), jnp.cos(angles)], axis=1)[:, None, :]
    sine = jnp.concatenate([jnp.sin(angles), jnp.sin(angles)], axis=1)[:, None, :]
    return (cosine, sine)


def causal_mask():
    counter = jnp.arange(SEQ, dtype=jnp.int32)
    return counter[:, None] >= counter[None, :]


def dot_full(left, right):
    return jnp.dot(left, right, precision=lax.Precision.HIGHEST, preferred_element_type=jnp.float32)


def norm_forward(source, gain):
    inverse_root = lax.rsqrt(jnp.mean(source * source, axis=1, keepdims=True) + EPSILON)
    return (inverse_root, source * inverse_root * gain)


def norm_backward(grad_in, source, inverse_root, gain):
    gain_grad = jnp.sum(grad_in * source * inverse_root, axis=0)
    scaled = grad_in * gain
    inner = jnp.mean(scaled * source, axis=1, keepdims=True)
    return (inverse_root * (scaled - source * inverse_root * inverse_root * inner), gain_grad)


def attend_forward(query, keys, values):
    scores = (
        jnp.einsum("sqkgd,stkd->skgqt", query, keys, preferred_element_type=jnp.float32)
        * SCORE_SCALE
    )
    scores = jnp.where(causal_mask(), scores, NEG_LARGE)
    highest = jnp.max(scores, axis=-1, keepdims=True)
    weights = jnp.exp(scores - highest)
    totals = jnp.sum(weights, axis=-1, keepdims=True)
    log_total = highest + jnp.log(totals)
    probability = (weights / totals).astype(jnp.bfloat16)
    attended = jnp.einsum(
        "skgqt,stkd->sqkgd", probability, values, preferred_element_type=jnp.float32
    )
    return (attended.astype(jnp.bfloat16), log_total)


def attend_backward(query, keys, values, attended, log_total, grad_out):
    scores = (
        jnp.einsum("sqkgd,stkd->skgqt", query, keys, preferred_element_type=jnp.float32)
        * SCORE_SCALE
    )
    scores = jnp.where(causal_mask(), scores, NEG_LARGE)
    probability = jnp.exp(scores - log_total)
    value_grad = jnp.einsum(
        "skgqt,sqkgd->stkd",
        probability.astype(jnp.bfloat16),
        grad_out,
        preferred_element_type=jnp.float32,
    )
    prob_grad = jnp.einsum(
        "sqkgd,stkd->skgqt", grad_out, values, preferred_element_type=jnp.float32
    )
    delta_rows = jnp.sum(grad_out.astype(jnp.float32) * attended.astype(jnp.float32), axis=-1)
    delta_rows = jnp.transpose(delta_rows, (0, 2, 3, 1))[..., None]
    score_grad = (probability * (prob_grad - delta_rows)).astype(jnp.bfloat16)
    query_grad = (
        jnp.einsum("skgqt,stkd->sqkgd", score_grad, keys, preferred_element_type=jnp.float32)
        * SCORE_SCALE
    )
    key_grad = (
        jnp.einsum("skgqt,sqkgd->stkd", score_grad, query, preferred_element_type=jnp.float32)
        * SCORE_SCALE
    )
    return (query_grad, key_grad, value_grad)


MESH = pl.DeviceIdType.MESH


def greet(devices):
    barrier = pltpu.get_barrier_semaphore()
    for device in devices:
        pl.semaphore_signal(barrier, inc=1, device_id=device, device_id_type=MESH)
    pl.semaphore_wait(barrier, len(devices))


def send(source, target, send_sem, recv_sem, device):
    copy = pltpu.make_async_remote_copy(
        src_ref=source,
        dst_ref=target,
        send_sem=send_sem,
        recv_sem=recv_sem,
        device_id=device,
        device_id_type=MESH,
    )
    copy.start()
    return copy


def span(start, size):
    return pl.ds(pl.multiple_of(start, size), size)


def places(n, t):
    me, z = lax.axis_index("dp"), lax.axis_index("tensor")
    core, chip = lax.rem(me, 2), lax.div(me, 2)
    chips = [lax.rem(chip + d, n // 2) for d in range(n // 2)]
    partner = (me + 1 - 2 * core, z)
    peers = [(2 * k + core, z) for k in chips]
    stacked = [(me, lax.rem(z + d, t)) for d in range(t)]
    return me, z, core, chips, partner, peers, stacked


def tensor_stages(t, rows, z, stacked, total, out_ref, slices, s3, r3, s4, r4):
    piece = rows // t
    shared, spread = {}, {}

    def share(c):
        for d in range(1, t):
            shared[c, d] = send(
                total.at[span(c * rows + stacked[d][1] * piece, piece)],
                slices.at[d - 1, span(c * piece, piece)],
                s3.at[c, d - 1],
                r3.at[c, d - 1],
                stacked[d],
            )

    def finish(c):
        mine = span(c * rows + z * piece, piece)
        value = total[mine].astype(jnp.float32)
        for d in range(1, t):
            shared[c, d].wait_recv()
            value = value + slices[d - 1, span(c * piece, piece)].astype(jnp.float32)
        out_ref[mine] = value.astype(out_ref.dtype)
        for d in range(1, t):
            spread[c, d] = send(
                out_ref.at[mine], out_ref.at[mine], s4.at[c, d - 1], r4.at[c, d - 1], stacked[d]
            )

    def drain(c):
        for d in range(1, t):
            spread[c, d].wait_recv()

    def settle():
        for copy in list(shared.values()) + list(spread.values()):
            copy.wait_send()

    return share, finish, drain, settle


def sum_kernel(n, t, chunks, part_ref, out_ref, slices, s3, r3, s4, r4):
    me, z, core, chips, partner, peers, stacked = places(n, t)
    rows = out_ref.shape[0] // chunks
    greet(stacked[1:])
    share, finish, drain, settle = tensor_stages(
        t, rows, z, stacked, part_ref, out_ref, slices, s3, r3, s4, r4
    )
    for c in range(chunks):
        share(c)
    for c in range(chunks):
        finish(c)
    for c in range(chunks):
        drain(c)
    settle()


def reduce_kernel(
    n, t, chunks, part_ref, out_ref, pairs, paired, arrived, total, slices, s1, r1, s2, r2, s3, r3, s4, r4
):
    me, z, core, chips, partner, peers, stacked = places(n, t)
    count = n // 2
    height = out_ref.shape[0]
    rows = height // chunks
    greet([partner] + peers[1:] + stacked[1:])
    share, finish, drain, settle = tensor_stages(
        t, rows, z, stacked, total, out_ref, slices, s3, r3, s4, r4
    )
    order = list(range(1, count)) + [0]
    crossed, passed = {}, {}
    for c in range(chunks):
        for d in order:
            crossed[c, d] = send(
                part_ref.at[span((2 * chips[d] + 1 - core) * height + c * rows, rows)],
                pairs.at[d, pl.ds(c * rows, rows)],
                s1.at[c, d],
                r1.at[c, d],
                partner,
            )

    def pair(c):
        here = pl.ds(c * rows, rows)
        for d in order:
            crossed[c, d].wait_recv()
            kept = part_ref[span((2 * chips[d] + core) * height + c * rows, rows)]
            value = kept.astype(jnp.float32) + pairs[d, here].astype(jnp.float32)
            paired[d, here] = value.astype(paired.dtype)
            if d:
                passed[c, d] = send(
                    paired.at[d, here],
                    arrived.at[d - 1, here],
                    s2.at[c, d - 1],
                    r2.at[c, d - 1],
                    peers[d],
                )

    def collect(c):
        here = pl.ds(c * rows, rows)
        value = paired[0, here].astype(jnp.float32)
        for d in range(1, count):
            passed[c, d].wait_recv()
            value = value + arrived[d - 1, here].astype(jnp.float32)
        total[here] = value.astype(total.dtype)
        share(c)

    for step in range(chunks + 3):
        for late, stage in enumerate((pair, collect, finish, drain)):
            if 0 <= step - late < chunks:
                stage(step - late)
    for copy in list(crossed.values()) + list(passed.values()):
        copy.wait_send()
    settle()


def gather_kernel(n, t, chunks, block_ref, out_ref, s1, r1, s2, r2, s3, r3, local_sem):
    me, z, core, chips, partner, peers, stacked = places(n, t)
    count = n // 2
    height = block_ref.shape[0]
    rows = height // chunks
    greet([partner] + peers[1:])
    direct, forward = {}, {}
    for c in range(chunks):
        for d in range(1, count):
            direct[c, d] = send(
                block_ref.at[pl.ds(c * rows, rows)],
                out_ref.at[span(me * height + c * rows, rows)],
                s1.at[c, d - 1],
                r1.at[c, d - 1],
                peers[d],
            )
    across = send(block_ref, out_ref.at[span(me * height, height)], s3, r3, partner)
    local = pltpu.make_async_copy(block_ref, out_ref.at[span(me * height, height)], local_sem)
    local.start()
    for c in range(chunks):
        for d in range(1, count):
            direct[c, d].wait_recv()
            place = span((2 * chips[count - d] + core) * height + c * rows, rows)
            forward[c, d] = send(
                out_ref.at[place], out_ref.at[place], s2.at[c, d - 1], r2.at[c, d - 1], partner
            )
    for copy in forward.values():
        copy.wait_recv()
    across.wait_recv()
    local.wait()
    for copy in list(direct.values()) + list(forward.values()) + [across]:
        copy.wait_send()


def comm_call(kernel, operand, out_rows, scratch, collective_id):
    n, t = lax.axis_size("dp"), lax.axis_size("tensor")
    chunks = max(SEQ // (16 * t), 1)
    return pl.pallas_call(
        functools.partial(kernel, n, t, chunks),
        out_shape=jax.ShapeDtypeStruct((out_rows, operand.shape[1]), operand.dtype),
        in_specs=[pl.BlockSpec(memory_space=pltpu.VMEM)],
        out_specs=pl.BlockSpec(memory_space=pltpu.VMEM),
        scratch_shapes=scratch(n, t, chunks, operand.shape[1]),
        compiler_params=pltpu.CompilerParams(collective_id=collective_id, has_side_effects=True),
    )(operand)


def twice(*shape):
    return [pltpu.SemaphoreType.DMA(shape), pltpu.SemaphoreType.DMA(shape)]


def sum_scratch(n, t, chunks, width):
    return (
        [pltpu.VMEM((t - 1, SEQ // t, width), jnp.bfloat16)]
        + twice(chunks, t - 1)
        + twice(chunks, t - 1)
    )


def reduce_scratch(n, t, chunks, width):
    half = n // 2
    return (
        [
            pltpu.VMEM((half, SEQ, width), jnp.bfloat16),
            pltpu.VMEM((half, SEQ, width), jnp.bfloat16),
            pltpu.VMEM((half - 1, SEQ, width), jnp.bfloat16),
            pltpu.VMEM((SEQ, width), jnp.bfloat16),
            pltpu.VMEM((t - 1, SEQ // t, width), jnp.bfloat16),
        ]
        + twice(chunks, half)
        + twice(chunks, half - 1)
        + twice(chunks, t - 1)
        + twice(chunks, t - 1)
    )


def gather_scratch(n, t, chunks, width):
    half = n // 2
    return (
        twice(chunks, half - 1)
        + twice(chunks, half - 1)
        + [pltpu.SemaphoreType.DMA] * 3
    )


def gather_rows(block):
    out_rows = block.shape[0] * lax.axis_size("dp")
    return comm_call(gather_kernel, block, out_rows, gather_scratch, 1)


def reduce_rows(partial, collective_id):
    out_rows = partial.shape[0] // lax.axis_size("dp")
    summed = comm_call(reduce_kernel, partial, out_rows, reduce_scratch, collective_id)
    return summed.astype(jnp.float32)


def sum_tensor(partial):
    partial = partial.astype(jnp.bfloat16)
    return comm_call(sum_kernel, partial, partial.shape[0], sum_scratch, 4).astype(jnp.float32)


def spread_columns(per_expert, hidden):
    count = per_expert.shape[1]
    return jnp.concatenate(
        [
            jnp.broadcast_to(per_expert[:, e : e + 1], (per_expert.shape[0], hidden))
            for e in range(count)
        ],
        axis=1,
    )


def layer_forward(inputs, params, local_chosen, cosine, sine):
    (
        attention_gain,
        query_weight,
        key_weight,
        value_weight,
        output_weight,
        mixture_gain,
        router_weight,
        gate_shard,
        up_shard,
        down_shard,
    ) = params
    row_count, width = inputs.shape
    query_heads = query_weight.shape[1] // HD
    key_heads = key_weight.shape[0] // HD
    group_size = query_heads // key_heads
    seq_count = row_count // SEQ
    local_experts, hidden, _ = gate_shard.shape
    first_scale, first_normed = norm_forward(inputs, attention_gain)
    first_input = first_normed.astype(jnp.bfloat16)
    query = jnp.dot(first_input, query_weight, preferred_element_type=jnp.float32).reshape(
        row_count, query_heads, HD
    )
    keys = jnp.dot(first_input, key_weight.T, preferred_element_type=jnp.float32).reshape(
        row_count, key_heads, HD
    )
    values = jnp.dot(first_input, value_weight.T, preferred_element_type=jnp.float32).astype(
        jnp.bfloat16
    )
    query = (query * cosine + rotate_half(query) * sine).astype(jnp.bfloat16)
    keys = (keys * cosine + rotate_half(keys) * sine).astype(jnp.bfloat16)
    query_split = query.reshape(seq_count, SEQ, key_heads, group_size, HD)
    key_split = keys.reshape(seq_count, SEQ, key_heads, HD)
    value_split = values.reshape(seq_count, SEQ, key_heads, HD)
    attended, log_total = attend_forward(query_split, key_split, value_split)
    attended_rows = attended.reshape(row_count, query_heads * HD)
    attention_out = sum_tensor(
        jnp.dot(attended_rows, output_weight, preferred_element_type=jnp.float32)
    )
    middle_state = inputs + RESIDUAL_SCALE * attention_out
    second_scale, second_normed = norm_forward(middle_state, mixture_gain)
    second_input = second_normed.astype(jnp.bfloat16)
    tokens = gather_rows(second_input)
    probs_all = jax.nn.softmax(
        jnp.dot(tokens, router_weight, preferred_element_type=jnp.float32), axis=1
    )
    first_expert = lax.axis_index("dp") * local_experts
    local_weights = local_chosen * lax.dynamic_slice_in_dim(
        probs_all, first_expert, local_experts, axis=1
    )
    weights = spread_columns(local_weights, hidden)
    gate_flat = gate_shard.reshape(local_experts * hidden, width)
    up_flat = up_shard.reshape(local_experts * hidden, width)
    down_flat = down_shard.reshape(local_experts * hidden, width)
    gate_pre = jnp.dot(tokens, gate_flat.T, preferred_element_type=jnp.float32)
    up_pre = jnp.dot(tokens, up_flat.T, preferred_element_type=jnp.float32)
    weighted = (weights * (jax.nn.silu(gate_pre) * up_pre)).astype(jnp.bfloat16)
    partial = jnp.dot(weighted, down_flat, preferred_element_type=jnp.float32).astype(jnp.bfloat16)
    outputs = middle_state + RESIDUAL_SCALE * reduce_rows(partial, 2)
    router_probs = jax.nn.softmax(
        jnp.dot(second_input, router_weight, preferred_element_type=jnp.float32), axis=1
    )
    saved = (
        first_scale,
        first_input,
        query_split,
        key_split,
        value_split,
        attended,
        log_total,
        middle_state,
        second_scale,
        second_input,
        router_probs,
        weights,
        tokens,
        gate_pre,
        up_pre,
        weighted,
    )
    return (outputs, saved)


def layer_backward(grad_out, grads, saved, params, chosen, cosine, sine, inputs):
    (
        attention_gain,
        query_weight,
        key_weight,
        value_weight,
        output_weight,
        mixture_gain,
        router_weight,
        gate_shard,
        up_shard,
        down_shard,
    ) = params
    (
        first_scale,
        first_input,
        query_split,
        key_split,
        value_split,
        attended,
        log_total,
        middle_state,
        second_scale,
        second_input,
        router_probs,
        weights,
        tokens,
        gate_pre,
        up_pre,
        weighted,
    ) = saved
    row_count, width = grad_out.shape
    query_heads = query_weight.shape[1] // HD
    key_heads = key_weight.shape[0] // HD
    local_experts, hidden, _ = gate_shard.shape
    expert_count = router_weight.shape[1]
    gate_flat = gate_shard.reshape(local_experts * hidden, width)
    up_flat = up_shard.reshape(local_experts * hidden, width)
    down_flat = down_shard.reshape(local_experts * hidden, width)
    if grads is None:
        grads = gather_rows((RESIDUAL_SCALE * grad_out).astype(jnp.bfloat16))
    back = jnp.dot(grads, down_flat.T, preferred_element_type=jnp.float32)
    sigma = jax.nn.sigmoid(gate_pre)
    products = gate_pre * sigma * up_pre * back
    weight_part = jnp.concatenate(
        [
            jnp.sum(products[:, e * hidden : (e + 1) * hidden], axis=1, keepdims=True)
            for e in range(local_experts)
        ],
        axis=1,
    )
    act_grad = weights * back
    gate_rows = (act_grad * up_pre * sigma * (1.0 + gate_pre * (1.0 - sigma))).astype(jnp.bfloat16)
    up_rows = (act_grad * gate_pre * sigma).astype(jnp.bfloat16)
    dispatch_part = jnp.dot(gate_rows, gate_flat, preferred_element_type=jnp.float32) + jnp.dot(
        up_rows, up_flat, preferred_element_type=jnp.float32
    )
    first_expert = lax.axis_index("dp") * local_experts
    side = lax.dynamic_update_slice_in_dim(
        jnp.zeros((tokens.shape[0], 128), jnp.float32), weight_part, first_expert, axis=1
    )
    summed = reduce_rows(
        jnp.concatenate([dispatch_part, side], axis=1).astype(jnp.bfloat16), 3
    )
    down_grad = jnp.dot(weighted.T, grads, preferred_element_type=jnp.float32)
    gate_grad = jnp.dot(gate_rows.T, tokens, preferred_element_type=jnp.float32)
    up_grad = jnp.dot(up_rows.T, tokens, preferred_element_type=jnp.float32)
    router_float = router_weight.astype(jnp.float32)
    prob_grad = chosen * summed[:, width : width + expert_count]
    logit_grad = router_probs * (
        prob_grad - jnp.sum(router_probs * prob_grad, axis=1, keepdims=True)
    )
    second_grad = summed[:, :width] + dot_full(logit_grad, router_float.T)
    router_grad = dot_full(second_input.astype(jnp.float32).T, logit_grad)
    middle_norm_grad, mixture_gain_grad = norm_backward(
        second_grad, middle_state, second_scale, mixture_gain
    )
    middle_grad = grad_out + middle_norm_grad
    attention_grad = (RESIDUAL_SCALE * middle_grad).astype(jnp.bfloat16)
    attended_rows = attended.reshape(row_count, query_heads * HD)
    output_grad = jnp.dot(attention_grad.T, attended_rows, preferred_element_type=jnp.float32)
    attended_grad = jnp.dot(
        attention_grad, output_weight.T, preferred_element_type=jnp.float32
    ).astype(jnp.bfloat16)
    query_grad, key_grad, value_grad = attend_backward(
        query_split,
        key_split,
        value_split,
        attended,
        log_total,
        attended_grad.reshape(attended.shape),
    )
    query_grad = query_grad.reshape(row_count, query_heads, HD)
    query_grad = (
        (query_grad * cosine - rotate_half(query_grad) * sine)
        .astype(jnp.bfloat16)
        .reshape(row_count, query_heads * HD)
    )
    key_grad = key_grad.reshape(row_count, key_heads, HD)
    key_grad = (
        (key_grad * cosine - rotate_half(key_grad) * sine)
        .astype(jnp.bfloat16)
        .reshape(row_count, key_heads * HD)
    )
    value_grad = value_grad.astype(jnp.bfloat16).reshape(row_count, key_heads * HD)
    first_part = (
        jnp.dot(query_grad, query_weight.T, preferred_element_type=jnp.float32)
        + jnp.dot(key_grad, key_weight, preferred_element_type=jnp.float32)
        + jnp.dot(value_grad, value_weight, preferred_element_type=jnp.float32)
    )
    first_grad = sum_tensor(first_part)
    input_norm_grad, attention_gain_grad = norm_backward(
        first_grad, inputs, first_scale, attention_gain
    )
    input_grad = middle_grad + input_norm_grad
    projected = jnp.dot(
        first_input.T,
        jnp.concatenate([query_grad, key_grad, value_grad], axis=1),
        preferred_element_type=jnp.float32,
    )
    small = jnp.concatenate(
        [
            router_grad,
            attention_gain_grad[:, None],
            mixture_gain_grad[:, None],
            jnp.zeros((width, 126 - expert_count), jnp.float32),
        ],
        axis=1,
    )
    dense = lax.psum_scatter(
        jnp.concatenate([projected, output_grad, small], axis=1).astype(jnp.bfloat16),
        "dp",
        scatter_dimension=0,
        tiled=True,
    ).astype(jnp.float32)
    q, k = query_heads * HD, key_heads * HD
    side = dense[:, 2 * q + 2 * k :]
    dense = (
        side[:, expert_count],
        dense[:, :q],
        dense[:, q : q + k].T,
        dense[:, q + k : q + 2 * k].T,
        dense[:, q + 2 * k : 2 * q + 2 * k].T,
        side[:, expert_count + 1],
        side[:, :expert_count],
    )
    experts = tuple(entry.reshape(gate_shard.shape) for entry in (gate_grad, up_grad, down_grad))
    return (input_grad, dense, experts)


def shards(
    hidden_states,
    output_cotangent,
    routes,
    attention_gain,
    query_weight,
    key_weight,
    value_weight,
    output_weight,
    mixture_gain,
    router_weight,
    gate_weight,
    up_weight,
    down_weight,
):
    params_all = (
        attention_gain,
        query_weight,
        key_weight,
        value_weight,
        output_weight,
        mixture_gain,
        router_weight,
        gate_weight,
        up_weight,
        down_weight,
    )
    row_count = hidden_states.shape[0]
    layer_count = query_weight.shape[0]
    cosine, sine = rope_tables(row_count)
    local_experts = gate_weight.shape[1]
    expert_ids = jnp.arange(EXPERTS, dtype=jnp.int32)
    chosen = jnp.any(routes[:, :, None] == expert_ids[None, None, :], axis=1).astype(jnp.float32)
    local_ids = lax.axis_index("dp") * local_experts + jnp.arange(local_experts, dtype=jnp.int32)
    routes_all = lax.all_gather(routes, "dp", axis=0, tiled=True)
    local_chosen = jnp.any(routes_all[:, :, None] == local_ids[None, None, :], axis=1).astype(
        jnp.float32
    )
    current = hidden_states
    kept = []
    for layer_index in range(layer_count):
        layer_params = tuple((weight[layer_index] for weight in params_all))
        layer_input = current
        current, saved = layer_forward(current, layer_params, local_chosen, cosine, sine)
        kept.append((saved, layer_input))
    grad_now = output_cotangent
    gathered = lax.all_gather(
        (RESIDUAL_SCALE * output_cotangent).astype(jnp.bfloat16), "dp", axis=0, tiled=True
    )
    dense_layers = [None] * layer_count
    expert_layers = [None] * layer_count
    for layer_index in reversed(range(layer_count)):
        layer_params = tuple((weight[layer_index] for weight in params_all))
        grad_now, dense, expert_grads = layer_backward(
            grad_now,
            gathered,
            kept[layer_index][0],
            layer_params,
            chosen,
            cosine,
            sine,
            kept[layer_index][1],
        )
        gathered = None
        dense_layers[layer_index] = dense
        expert_layers[layer_index] = expert_grads
    stacked = tuple(
        (jnp.stack([entry[position] for entry in dense_layers]) for position in range(7))
    )
    experts_stacked = tuple(
        (jnp.stack([entry[position] for entry in expert_layers]) for position in range(3))
    )
    return (
        current,
        grad_now,
        stacked[0],
        stacked[1],
        stacked[2],
        stacked[3],
        stacked[4],
        stacked[5],
        stacked[6],
        experts_stacked[0],
        experts_stacked[1],
        experts_stacked[2],
    )


def solution(mesh):
    placed = (
        P("dp", None),
        P("dp", None),
        P("dp", None),
        P(),
        P(None, None, "tensor"),
        P(None, "tensor", None),
        P(None, "tensor", None),
        P(None, "tensor", None),
        P(),
        P(),
        P(None, "dp", "tensor", None),
        P(None, "dp", "tensor", None),
        P(None, "dp", "tensor", None),
    )
    return jax.shard_map(
        shards,
        mesh=mesh,
        in_specs=placed,
        out_specs=(
            P("dp", None),
            P("dp", None),
            P(None, "dp"),
            P(None, "dp", "tensor"),
            P(None, "tensor", "dp"),
            P(None, "tensor", "dp"),
            P(None, "tensor", "dp"),
            P(None, "dp"),
            P(None, "dp", None),
            P(None, "dp", "tensor", None),
            P(None, "dp", "tensor", None),
            P(None, "dp", "tensor", None),
        ),
        check_vma=False,
    )
```

time: 1470 us -> 696 us (0.47)
  waiting for transfers between devices: 774 us -> 17 us
  Pallas kernels: 0 us -> 381 us
  blocking collectives: 193 us -> 10.9 us
  local copies, waits for them, and re-layouts: 218 us -> 58.3 us
  other arithmetic: 127 us -> 61.7 us
  matrix products: 102 us -> 140 us
  starting transfers between devices: 31 us -> 0.12 us
    pallas_call x0 -> x11, Pallas kernels: none -> 381 us  [comm_call(): pl.pallas_call(functools.partial(kernel, n, t, chunks), out_shape=jax.Sha...]
    all_to_all x6 -> x0, waiting for transfers between devices: 353 us -> none  [the longest x2 124 us: layer_forward(): lax.all_to_all(partial_out.astype(jnp.bfloat16), 'dp', split_axis=1, conc...]
    psum x7 -> x0, waiting for transfers between devices: 204 us -> none  [the longest x2 96 us: layer_forward(): lax.psum(jnp.dot(attended_rows, output_weight, preferred_element_type=jnp...]
    unnamed x20 -> x5, waiting for transfers between devices: 179 us -> 17 us
    all_to_all x2 -> x0, blocking collectives: 151 us -> none  [the longest x1 75.7 us: layer_forward(): lax.all_to_all(dispatched, 'dp', split_axis=0, concat_axis=1, tiled=True)]
    convert_element_type x8 -> x0, local copies, waits for them, and re-layouts: 80.1 us -> none  [the longest x2 20.8 us: layer_forward(): partial_out.astype(jnp.bfloat16)]
    gather x4 -> x0, local copies, waits for them, and re-layouts: 65.3 us -> none  [the longest x2 32.6 us: layer_backward(): input_part = jnp.sum(dispatch_grad[targets], axis=1)]
    psum x2 -> x0, blocking collectives: 42.2 us -> none  [layer_backward(): weight_grad = lax.psum(weight_part, 'tensor')]
  transfers between devices with their start and end apart: 20 -> 3, of which waited for: 20 -> 1; matrix products, arithmetic and copies ran while one was open for 12% -> 16% of each run, Pallas kernels for 0% -> 27%
where the time goes in v1:
time: 696 us; the launch traced here: 685 us
  Pallas kernels  381 us (55%)
  matrix products  140 us (20%)
  other arithmetic  61.7 us (9%)
  local copies, waits for them, and re-layouts  58.3 us (8%)
  waiting for transfers between devices  17 us (2%)
  between operations  16.2 us (2%)
  blocking collectives  10.9 us (2%)
    pallas_call x11, Pallas kernels, comm_call(): pl.pallas_call(functools.partial(kernel, n, t, chunks), out_shape=jax.Sha...  381 us
    unnamed x285, local copies, waits for them, and re-layouts  21.3 us
    unnamed x5, waiting for transfers between devices  17 us
    dot_general x2, matrix products, layer_backward(): back = jnp.dot(grads, down_flat.T, preferred_element_type=jnp.float32)  16.6 us
  transfers between devices with their start and end apart: 3, of which 1 were waited for; matrix products, arithmetic and copies ran while one was open for 16% of the time, Pallas kernels for 27%

profile of v1, /device:TPU:0, one launch (start us, length us, event | category | flops | bytes accessed | tf_op | source)
XLA Modules:
  0.0 685.4 jit_solution(898464108913190143)
XLA Ops:
  7.2 2.3 multiply_convert_fusion.7
  13.2 10.9 %all_gather.6 = s32[2048,8]{0,1:T(8,128)S(1)} all-gather(s32[256,8]{0,1:T(8,128)} %param.15), channel_id=1, replica_groups=mesh['dp'=8,'tensor'=4] {'dp'}, dimensions={0}, use_global_device_ids=true | all-gather | bytes 73728 | tf_op jit(solution)/shard_map/all_gather | solution.py:634
  24.0 1.8 fusion.169
  26.0 2.1 convolution_convert_fusion.15
  34.3 29.2 %shard_map.220 = bf16[256,1024]{1,0:T(8,128)(2,1)} custom-call(bf16[256,1024]{1,0:T(8,128)(2,1)} %convolution_convert_fusion.7.part_ref), custom_call_target="tpu_custom_call" | custom-call | tf_op jit(solution)/shard_map/pallas_call | solution.py:291
  63.6 1.4 multiply_reduce_fusion.6
  65.1 3.2 fusion.166
  69.4 1.6 fusion.168
  72.0 30.5 %shard_map.221 = bf16[2048,1024]{1,0:T(8,128)(2,1)} custom-call(bf16[256,1024]{1,0:T(8,128)(2,1)} %multiply_convert_fusion.10.block_ref), custom_call_target="tpu_custom_call" | custom-call | tf_op jit(solution)/shard_map/pallas_call | solution.py:291
  102.7 3.7 fusion.175
  106.5 2.4 fusion.181
  108.9 2.4 fusion.180
  111.8 1.5 copy-done.73
  113.3 4.4 convolution_convert_fusion.1.part_ref
  119.8 42.6 %shard_map.222 = bf16[256,1024]{1,0:T(8,128)(2,1)} custom-call(bf16[2048,1024]{1,0:T(8,128)(2,1)} %convolution_convert_fusion.1.part_ref), custom_call_target="tpu_custom_call" | custom-call | tf_op jit(solution)/shard_map/pallas_call | solution.py:291
  170.0 26.7 %shard_map.223 = bf16[256,1024]{1,0:T(8,128)(2,1)} custom-call(bf16[256,1024]{1,0:T(8,128)(2,1)} %convolution_convert_fusion.6.part_ref), custom_call_target="tpu_custom_call" | custom-call | tf_op jit(solution)/shard_map/pallas_call | solution.py:291
  199.8 30.0 %shard_map.224 = bf16[2048,1024]{1,0:T(8,128)(2,1)} custom-call(bf16[256,1024]{1,0:T(8,128)(2,1)} %multiply_convert_fusion.8.block_ref), custom_call_target="tpu_custom_call" | custom-call | tf_op jit(solution)/shard_map/pallas_call | solution.py:291
  229.8 1.9 fusion.178
  232.6 1.5 fusion.120
  236.8 3.5 fusion.177
  240.5 4.4 fusion.182
  244.9 7.0 %fusion.183 = f32[2048,512]{0,1:T(8,128)} fusion(bf16[2048,1024]{1,0:T(8,128)(2,1)} %all-gather.2.cloned.1.call-done, bf16[512,1024]{1,0:T(8,128)(2,1)} %bitcast.460), kind=kOutput, calls=%fused_computation.352 | convolution fusion | flops 2147483648 | bytes 9437184 | tf_op jit(solution)/shard_map/dot_general | solution.py:491
  252.3 2.9 copy-done.7
  255.2 9.2 %multiply_convert_fusion.2 = (bf16[2048,512]{0,1:T(8,128)(2,1)}, bf16[2048,512]{0,1:T(8,128)(2,1)}, f32[2048,512]{0,1:T(8,128)S(1)}, f32[2048,512]{0,1:T(8,128)}) fusion(f32[2048,512]{0,1:T(8,128)} %fusion.183, f32[2048,128]{0,1:T(8,128)S(1)} %broadcast_in_dim.169, f32[2048,128]{0,1:T(8,128)S(1)} %broadcast_in_dim.167, ...), kind=kOutput, calls=%fused_computation.17 | convolution fusion | flops 2168455168 | bytes 30408704 | tf_op jit(solution)/shard_map/dot_general | solution.py:421
  265.9 6.6 fusion.189
  272.6 2.4 fusion.184
  275.0 4.6 add_convert_fusion.1
  280.5 5.4 dynamic_update_slice.6
  285.9 5.1 pad_maximum_fusion.part_ref
  291.0 46.8 %shard_map.226 = bf16[256,1152]{1,0:T(8,128)(2,1)} custom-call(bf16[2048,1152]{1,0:T(8,128)(2,1)} %pad_maximum_fusion.part_ref), custom_call_target="tpu_custom_call" | custom-call | tf_op jit(solution)/shard_map/pallas_call | solution.py:291
  340.5 2.2 convolution_convert_fusion.12
  342.8 3.1 multiply_reduce_fusion
  345.9 8.4 %convolution_convert_fusion.part_ref = bf16[2048,1024]{1,0:T(8,128)(2,1)} fusion(bf16[512,1024]{1,0:T(8,128)(2,1)S(1)} %bitcast.461, f32[2048,128]{0,1:T(8,128)S(1)} %copy-done.62, f32[2048,128]{0,1:T(8,128)S(1)} %copy-done.66, f32[2048,128]{0,1:T(8,128)S(1)} %copy-done.68, f32[2048,128]{0,1:T(8,128)S(1)} %copy-done.64, f32[2048,512]{0,1:T(8,128)} %fusion.182, ...), kind=kOutput, calls=%fused_computation.23 | convolution fusion | flops 2160066560 | bytes 17825792 | tf_op jit(solution)/shard_map/dot_general | solution.py:424
  354.3 42.1 %shard_map.225 = bf16[256,1024]{1,0:T(8,128)(2,1)} custom-call(bf16[2048,1024]{1,0:T(8,128)(2,1)} %convolution_convert_fusion.part_ref), custom_call_target="tpu_custom_call" | custom-call | tf_op jit(solution)/shard_map/pallas_call | solution.py:291
  396.6 3.5 multiply_add_fusion.1
  406.9 28.6 %shard_map.227 = bf16[256,1024]{1,0:T(8,128)(2,1)} custom-call(bf16[256,1024]{1,0:T(8,128)(2,1)} %fusion.14.part_ref), custom_call_target="tpu_custom_call" | custom-call | tf_op jit(solution)/shard_map/pallas_call | solution.py:291
  435.6 2.0 fusion.35
  437.6 2.3 multiply_convert_fusion.5.block_ref
  439.9 29.8 %shard_map.228 = bf16[2048,1024]{1,0:T(8,128)(2,1)} custom-call(bf16[256,1024]{1,0:T(8,128)(2,1)} %multiply_convert_fusion.5.block_ref), custom_call_target="tpu_custom_call" | custom-call | tf_op jit(solution)/shard_map/pallas_call | solution.py:291
  469.8 9.6 %multiply_convert_fusion = (bf16[2048,512]{0,1:T(8,128)(2,1)}, bf16[2048,512]{0,1:T(8,128)(2,1)}, f32[2048,512]{0,1:T(8,128)S(1)}) fusion(f32[2048,512]{0,1:T(8,128)} %copy-done.138, f32[2048,128]{0,1:T(8,128)} %copy-done.53, f32[2048,128]{0,1:T(8,128)} %copy-done.57, f32[2048,128]{0,1:T(8,128)} %copy-done.59, f32[2048,128]{0,1:T(8,128)} %copy-done.55, ...), kind=kOutput, calls=%fused_computation.15 | convolution fusion | flops 2168455168 | bytes 26214400 | tf_op jit(solution)/shard_map/dot_general | solution.py:491
  480.3 1.8 copy.106
  482.1 7.6 %fusion.185 = f32[2048,1024]{1,0:T(8,128)} fusion(bf16[2048,512]{0,1:T(8,128)(2,1)} %get-tuple-element.85, bf16[512,1024]{1,0:T(8,128)(2,1)} %bitcast.456), kind=kOutput, calls=%fused_computation.354 | convolution fusion | flops 2147483648 | bytes 11534336 | tf_op jit(solution)/shard_map/dot_general | solution.py:504
  490.5 5.2 dynamic_update_slice.7
  495.8 6.8 add_convert_fusion
  502.6 2.7 pad_maximum_fusion.1.part_ref
  505.3 47.2 %shard_map.229 = bf16[256,1152]{1,0:T(8,128)(2,1)} custom-call(bf16[2048,1152]{1,0:T(8,128)(2,1)} %pad_maximum_fusion.1.part_ref), custom_call_target="tpu_custom_call" | custom-call | tf_op jit(solution)/shard_map/pallas_call | solution.py:291
  554.9 2.3 convolution_convert_fusion.13
  557.2 2.5 multiply_reduce_fusion.1
  568.8 3.4 concatenate.117
  572.3 2.5 copy.135
  578.0 27.1 %shard_map.230 = bf16[256,1024]{1,0:T(8,128)(2,1)} custom-call(bf16[256,1024]{1,0:T(8,128)(2,1)} %fusion.15.part_ref), custom_call_target="tpu_custom_call" | custom-call | tf_op jit(solution)/shard_map/pallas_call | solution.py:291
  605.1 2.4 convolution_convert_fusion.3
  608.9 5.3 concatenate.114
  614.2 2.5 copy.133
  616.7 5.3 fusion.187
  622.1 3.7 fusion.186
  625.8 1.7 copy-done.137
  628.6 4.9 fusion.159
  633.6 8.0 %fusion.156 = f32[512,1024]{1,0:T(8,128)S(1)} fusion(bf16[2048,1024]{1,0:T(8,128)(2,1)} %all-gather.2.cloned.1.call-done, f32[2048,128]{0,1:T(8,128)} %copy-done.61, f32[2048,128]{0,1:T(8,128)} %copy-done.65, f32[2048,128]{0,1:T(8,128)} %copy-done.67, f32[2048,128]{0,1:T(8,128)} %copy-done.63, f32[2048,512]{0,1:T(8,128)} %fusion.182, ...), kind=kOutput, calls=%fused_computation.329 | convolution fusion | flops 2157969408 | bytes 18874368 | tf_op jit(solution)/shard_map/dot_general | solution.py:514
  641.6 2.3 pad_maximum_fusion.6
  644.2 2.5 pad_maximum_fusion.4
  648.6 2.3 fusion.188
  651.0 2.3 pad_maximum_fusion.5
  655.8 17.0 %reduce-scatter.7.cloned.1.call-done = bf16[128,896]{1,0:T(8,128)(2,1)} async-done(((bf16[1024,896]{1,0:T(8,128)(2,1)}), bf16[128,896]{1,0:T(8,128)(2,1)}) %reduce-scatter.7.cloned.1.call-update) | async-done | bytes 229392
  (431 shorter events, 70.2 us)
Async XLA Ops:
  7.2 18.6 %copy-start = (f32[256,1024]{1,0:T(8,128)S(1)}, f32[256,1024]{1,0:T(8,128)}, u32[]{:S(2)}) copy-start(f32[256,1024]{1,0:T(8,128)} %param.13) | copy-start | bytes 3145732
  7.2 21.8 %copy-start.20 = (bf16[2,1024,256]{2,1,0:T(8,128)(2,1)S(1)}, bf16[2,1024,256]{2,1,0:T(8,128)(2,1)}, u32[]{:S(2)}) copy-start(bf16[2,1024,256]{2,1,0:T(8,128)(2,1)} %param.17) | copy-start | bytes 3145732
  7.2 237.7 %all-gather.2.cloned.1.call-start = ((), (), s32[]{:S(2)}) async-start(), calls=%async_computation.2 | async-start | bytes 4718592 | tf_op jit(solution)/shard_map/all_gather | solution.py:646
  9.5 645.1 %reduce-scatter.9.cloned.1.call-start = ((), (), s32[]{:S(2)}) async-start(), calls=%async_computation.4 | async-start | bytes 2064384
  11.5 18.9 %copy-start.117 = (f32[256]{0:T(256)}, f32[256]{0:T(256)S(1)}, u32[]{:S(2)}) copy-start(f32[256]{0:T(256)S(1)} %add_rsqrt_fusion.3) | copy-start | bytes 3076
  12.3 18.1 %copy-start.102 = (f32[1,1024]{1,0:T(1,128)}, f32[1,1024]{1,0:T(1,128)S(1)}, u32[]{:S(2)}) copy-start(f32[1,1024]{1,0:T(1,128)S(1)} %get-tuple-element.160) | copy-start | bytes 12292
  13.1 57.9 %copy-start.109 = (f32[1,1024]{1,0:T(1,128)}, f32[1,1024]{1,0:T(1,128)S(1)}, u32[]{:S(2)}) copy-start(f32[1,1024]{1,0:T(1,128)S(1)} %get-tuple-element.159) | copy-start | bytes 12292
  13.1 185.0 %copy-start.107 = (f32[1,1024]{1,0:T(1,128)}, f32[1,1024]{1,0:T(1,128)S(1)}, u32[]{:S(2)}) copy-start(f32[1,1024]{1,0:T(1,128)S(1)} %get-tuple-element.158) | copy-start | bytes 12292
  32.3 31.3 %copy-start.44 = (bf16[256,4,64]{0,2,1:T(8,128)(2,1)}, bf16[256,4,64]{0,2,1:T(8,128)(2,1)S(1)}, u32[]{:S(2)}) copy-start(bf16[256,4,64]{0,2,1:T(8,128)(2,1)S(1)} %fusion.75) | copy-start | bytes 393220
  32.7 32.4 %copy-start.104 = (f32[2,2,256]{2,1,0:T(2,128)}, f32[2,2,256]{2,1,0:T(2,128)S(1)}, u32[]{:S(2)}) copy-start(f32[2,2,256]{2,1,0:T(2,128)S(1)} %get-tuple-element.164) | copy-start | bytes 12292
  32.9 32.2 %copy-start.115 = (f32[2,2,256]{2,1,0:T(2,128)}, f32[2,2,256]{2,1,0:T(2,128)S(1)}, u32[]{:S(2)}) copy-start(f32[2,2,256]{2,1,0:T(2,128)S(1)} %fusion.38) | copy-start | bytes 12292
  33.2 35.1 %copy-start.48 = (bf16[2,64,2,256]{3,1,2,0:T(8,128)(2,1)}, bf16[2,64,2,256]{3,1,2,0:T(8,128)(2,1)S(1)}, u32[]{:S(2)}) copy-start(bf16[2,64,2,256]{3,1,2,0:T(8,128)(2,1)S(1)} %convolution_convert_fusion.11) | copy-start | bytes 393220
  65.1 6.0 copy-start.121
  69.4 37.1 %copy-start.71 = (bf16[1,4,128,1024]{3,2,1,0:T(8,128)(2,1)}, bf16[1,4,128,1024]{3,2,1,0:T(8,128)(2,1)S(1)}, u32[]{:S(2)}) copy-start(bf16[1,4,128,1024]{3,2,1,0:T(8,128)(2,1)S(1)} %get-tuple-element.93) | copy-start | bytes 3145732
  71.0 31.4 %copy-start.131 = (s32[4]{0:T(128)S(1)}, s32[4]{0:T(128)}, u32[]{:S(2)}) copy-start(s32[4]{0:T(128)} %iota_add_fusion) | copy-start | bytes 52
  71.0 31.6 %copy-start.86 = (bf16[2,1024,32]{1,2,0:T(8,128)(2,1)S(1)}, bf16[2,1024,32]{1,2,0:T(8,128)(2,1)}, u32[]{:S(2)}) copy-start(bf16[2,1024,32]{1,2,0:T(8,128)(2,1)} %param.22) | copy-start | bytes 393220
  111.3 6.5 copy-start.138
  111.4 6.4 copy-start.53
  111.5 6.3 copy-start.55
  111.6 6.2 copy-start.57
  113.3 5.5 copy-start.18
  119.7 112.9 %copy-start.41 = (f32[256,32]{1,0:T(8,128)}, f32[256,32]{1,0:T(8,128)S(1)}, u32[]{:S(2)}) copy-start(f32[256,32]{1,0:T(8,128)S(1)} %copy.107) | copy-start | bytes 98308
  119.7 45.3 %copy-start.69 = (bf16[1,128,1024]{2,1,0:T(8,128)(2,1)S(1)}, bf16[1,128,1024]{2,1,0:T(8,128)(2,1)}, u32[]{:S(2)}) copy-start(bf16[1,128,1024]{2,1,0:T(8,128)(2,1)} %get-tuple-element.100) | copy-start | bytes 786436
  166.9 29.8 %copy-start.2 = (bf16[256,1024]{1,0:T(8,128)(2,1)S(1)}, bf16[256,1024]{1,0:T(8,128)(2,1)}, u32[]{:S(2)}) copy-start(bf16[256,1024]{1,0:T(8,128)(2,1)} %shard_map.222) | copy-start | bytes 1572868
  196.7 33.1 %copy-start.87 = (bf16[2,1024,32]{1,2,0:T(8,128)(2,1)S(1)}, bf16[2,1024,32]{1,2,0:T(8,128)(2,1)}, u32[]{:S(2)}) copy-start(bf16[2,1024,32]{1,2,0:T(8,128)(2,1)} %param.22) | copy-start | bytes 393220
  198.2 144.6 %copy-start.14 = (f32[256,1024]{1,0:T(8,128)}, f32[256,1024]{1,0:T(8,128)S(1)}, u32[]{:S(2)}) copy-start(f32[256,1024]{1,0:T(8,128)S(1)} %get-tuple-element.79) | copy-start | bytes 3145732
  232.6 7.9 %copy-start.6 = (bf16[2048,1024]{1,0:T(8,128)(2,1)S(1)}, bf16[2048,1024]{1,0:T(8,128)(2,1)}, u32[]{:S(2)}) copy-start(bf16[2048,1024]{1,0:T(8,128)(2,1)} %shard_map.224) | copy-start | bytes 12582916
  232.6 7.9 %copy-start.77 = (bf16[1,4,128,1024]{3,2,1,0:T(8,128)(2,1)S(1)}, bf16[1,4,128,1024]{3,2,1,0:T(8,128)(2,1)}, u32[]{:S(2)}) copy-start(bf16[1,4,128,1024]{3,2,1,0:T(8,128)(2,1)} %get-tuple-element.92) | copy-start | bytes 3145732
  244.9 7.4 %copy-start.75 = (bf16[1,4,128,1024]{3,2,1,0:T(8,128)(2,1)S(1)}, bf16[1,4,128,1024]{3,2,1,0:T(8,128)(2,1)}, u32[]{:S(2)}) copy-start(bf16[1,4,128,1024]{3,2,1,0:T(8,128)(2,1)} %get-tuple-element.90) | copy-start | bytes 3145732
  252.0 12.5 %copy-start.61 = (f32[2048,128]{0,1:T(8,128)}, f32[2048,128]{0,1:T(8,128)S(1)}, u32[]{:S(2)}) copy-start(f32[2048,128]{0,1:T(8,128)S(1)} %broadcast_in_dim.169) | copy-start | bytes 3145732
  252.1 12.4 %copy-start.63 = (f32[2048,128]{0,1:T(8,128)}, f32[2048,128]{0,1:T(8,128)S(1)}, u32[]{:S(2)}) copy-start(f32[2048,128]{0,1:T(8,128)S(1)} %broadcast_in_dim.163) | copy-start | bytes 3145732
  252.2 12.3 %copy-start.65 = (f32[2048,128]{0,1:T(8,128)}, f32[2048,128]{0,1:T(8,128)S(1)}, u32[]{:S(2)}) copy-start(f32[2048,128]{0,1:T(8,128)S(1)} %broadcast_in_dim.167) | copy-start | bytes 3145732
  255.2 9.3 %copy-start.67 = (f32[2048,128]{0,1:T(8,128)}, f32[2048,128]{0,1:T(8,128)S(1)}, u32[]{:S(2)}) copy-start(f32[2048,128]{0,1:T(8,128)S(1)} %broadcast_in_dim.165) | copy-start | bytes 3145732
  265.9 6.6 copy-start.76
  265.9 6.6 copy-start.132
  291.0 48.2 %copy-start.120 = (f32[256]{0:T(256)S(1)}, f32[256]{0:T(256)}, u32[]{:S(2)}) copy-start(f32[256]{0:T(256)} %copy-done.119) | copy-start | bytes 3076
  291.0 51.8 %copy-start.88 = (bf16[2,1024,32]{1,2,0:T(8,128)(2,1)S(1)}, bf16[2,1024,32]{1,2,0:T(8,128)(2,1)}, u32[]{:S(2)}) copy-start(bf16[2,1024,32]{1,2,0:T(8,128)(2,1)} %param.22) | copy-start | bytes 393220
  291.0 51.8 %copy-start.108 = (f32[1,1024]{1,0:T(1,128)S(1)}, f32[1,1024]{1,0:T(1,128)}, u32[]{:S(2)}) copy-start(f32[1,1024]{1,0:T(1,128)} %copy-done.107) | copy-start | bytes 12292
  337.8 8.1 %copy-start.62 = (f32[2048,128]{0,1:T(8,128)S(1)}, f32[2048,128]{0,1:T(8,128)}, u32[]{:S(2)}) copy-start(f32[2048,128]{0,1:T(8,128)} %copy-done.61) | copy-start | bytes 3145732
  337.8 8.1 %copy-start.64 = (f32[2048,128]{0,1:T(8,128)S(1)}, f32[2048,128]{0,1:T(8,128)}, u32[]{:S(2)}) copy-start(f32[2048,128]{0,1:T(8,128)} %copy-done.63) | copy-start | bytes 3145732
  337.8 8.1 %copy-start.66 = (f32[2048,128]{0,1:T(8,128)S(1)}, f32[2048,128]{0,1:T(8,128)}, u32[]{:S(2)}) copy-start(f32[2048,128]{0,1:T(8,128)} %copy-done.65) | copy-start | bytes 3145732
  337.8 8.1 %copy-start.68 = (f32[2048,128]{0,1:T(8,128)S(1)}, f32[2048,128]{0,1:T(8,128)}, u32[]{:S(2)}) copy-start(f32[2048,128]{0,1:T(8,128)} %copy-done.67) | copy-start | bytes 3145732
  337.9 8.1 %copy-start.74 = (bf16[1,4,128,1024]{3,2,1,0:T(8,128)(2,1)S(1)}, bf16[1,4,128,1024]{3,2,1,0:T(8,128)(2,1)}, u32[]{:S(2)}) copy-start(bf16[1,4,128,1024]{3,2,1,0:T(8,128)(2,1)} %get-tuple-element.94) | copy-start | bytes 3145732
  354.3 42.2 %copy-start.130 = (f32[256]{0:T(256)S(1)}, f32[256]{0:T(256)}, u32[]{:S(2)}) copy-start(f32[256]{0:T(256)} %get-tuple-element.71) | copy-start | bytes 3076
  354.3 42.2 %copy-start.124 = (f32[256]{0:T(256)S(1)}, f32[256]{0:T(256)}, u32[]{:S(2)}) copy-start(f32[256]{0:T(256)} %copy-done.123) | copy-start | bytes 3076
  404.3 31.3 %copy-start.113 = (f32[256]{0:T(256)S(1)}, f32[256]{0:T(256)}, u32[]{:S(2)}) copy-start(f32[256]{0:T(256)} %copy-done.112) | copy-start | bytes 3076
  437.6 32.1 %copy-start.125 = (f32[256]{0:T(256)}, f32[256]{0:T(256)S(1)}, u32[]{:S(2)}) copy-start(f32[256]{0:T(256)S(1)} %broadcast_multiply_fusion.9) | copy-start | bytes 3076
  495.8 6.8 copy-start.29
  505.3 51.9 %copy-start.110 = (f32[1,1024]{1,0:T(1,128)S(1)}, f32[1,1024]{1,0:T(1,128)}, u32[]{:S(2)}) copy-start(f32[1,1024]{1,0:T(1,128)} %copy-done.109) | copy-start | bytes 12292
  552.5 7.2 %copy-start.17 = (bf16[256,1024]{1,0:T(8,128)(2,1)S(1)}, bf16[256,1024]{1,0:T(8,128)(2,1)}, u32[]{:S(2)}) copy-start(bf16[256,1024]{1,0:T(8,128)(2,1)} %shard_map.227) | copy-start | bytes 1572868
  552.5 7.2 %copy-start.114 = (f32[256]{0:T(256)S(1)}, f32[256]{0:T(256)}, u32[]{:S(2)}) copy-start(f32[256]{0:T(256)} %copy-done.112) | copy-start | bytes 3076
  552.5 7.2 %copy-start.122 = (f32[256]{0:T(256)S(1)}, f32[256]{0:T(256)}, u32[]{:S(2)}) copy-start(f32[256]{0:T(256)} %copy-done.121) | copy-start | bytes 3076
  552.5 7.2 %copy-start.126 = (f32[256]{0:T(256)S(1)}, f32[256]{0:T(256)}, u32[]{:S(2)}) copy-start(f32[256]{0:T(256)} %copy-done.125) | copy-start | bytes 3076
  574.8 30.3 %copy-start.16 = (bf16[256,1024]{1,0:T(8,128)(2,1)S(1)}, bf16[256,1024]{1,0:T(8,128)(2,1)}, u32[]{:S(2)}) copy-start(bf16[256,1024]{1,0:T(8,128)(2,1)} %copy-done.15) | copy-start | bytes 1572868
  574.8 98.0 %reduce-scatter.7.cloned.1.call-start = ((), (), s32[]{:S(2)}) async-start(), calls=%async_computation.3 | async-start | bytes 2064384
  575.3 32.2 %copy-start.1 = (f32[256,1024]{1,0:T(8,128)S(1)}, f32[256,1024]{1,0:T(8,128)}, u32[]{:S(2)}) copy-start(f32[256,1024]{1,0:T(8,128)} %param.13) | copy-start | bytes 3145732
  575.3 32.2 %copy-start.103 = (f32[1,1024]{1,0:T(1,128)S(1)}, f32[1,1024]{1,0:T(1,128)}, u32[]{:S(2)}) copy-start(f32[1,1024]{1,0:T(1,128)} %copy-done.102) | copy-start | bytes 12292
  575.3 32.2 %copy-start.118 = (f32[256]{0:T(256)S(1)}, f32[256]{0:T(256)}, u32[]{:S(2)}) copy-start(f32[256]{0:T(256)} %copy-done.117) | copy-start | bytes 3076
  575.7 33.1 %copy-start.129 = (bf16[1024]{0:T(1024)(128)(2,1)S(1)}, bf16[1024]{0:T(1024)(128)(2,1)}, u32[]{:S(2)}) copy-start(bf16[1024]{0:T(1024)(128)(2,1)} %get-tuple-element.68) | copy-start | bytes 6148
  575.7 33.2 %copy-start.28 = (bf16[1024,256]{0,1:T(8,128)(2,1)S(1)}, bf16[1024,256]{0,1:T(8,128)(2,1)}, u32[]{:S(2)}) copy-start(bf16[1024,256]{0,1:T(8,128)(2,1)} %convolution_convert_fusion.5) | copy-start | bytes 1572868
  576.8 32.1 %copy-start.97 = (bf16[1024,32]{0,1:T(8,128)(2,1)S(1)}, bf16[1024,32]{0,1:T(8,128)(2,1)}, u32[]{:S(2)}) copy-start(bf16[1024,32]{0,1:T(8,128)(2,1)} %convolution_convert_fusion.13) | copy-start | bytes 196612
  622.1 5.4 copy-start.137
  622.1 6.6 copy-start.139
  633.6 8.0 %copy-start.37 = (f32[512,1024]{1,0:T(8,128)S(1)}, f32[512,1024]{1,0:T(8,128)}, u32[]{:S(2)}) copy-start(f32[512,1024]{1,0:T(8,128)} %fusion.159) | copy-start | bytes 6291460
  (79 other events, 253.4 us)
Sparse Core Ops, SparseCore 0:
  10.5 39.2 all-gather.1
  574.9 38.6 reduce-scatter.8
  633.7 39.0 reduce-scatter.6
